TPU v7x, 128 devices: a whole 4x4x4 slice. The times are simulated.
128 devices in a mesh: sect: 2 (over core), exp: 16 (over y, x), tp: 4 (over z).
Axes of the slice: x: 4, y: 4, z: 4, core: 2. Of those that a mesh axis runs over, the one named last changes fastest.
Arguments:
- tokens: bfloat16 [1024, 6144], P(('sect', 'exp', 'tp')), may hold values from -6 to 6
- router_logits: float32 [1024, 2], P(('sect', 'exp', 'tp')), may hold values from -6 to 6
- expert_ids: int32 [1024, 2], P(('sect', 'exp', 'tp')), may hold values from 0 to 7, all different within a row; in each aligned block of 8 rows (0 to 7, 8 to 15, ...) at most 4 rows name the same one
- w_gate: bfloat16 [32, 6144, 2048], P(('sect', 'exp'), None, 'tp'), may hold values from -0.078125 to 0.078125
- w_up: bfloat16 [32, 6144, 2048], P(('sect', 'exp'), None, 'tp'), may hold values from -0.078125 to 0.078125
- w_down: bfloat16 [32, 2048, 6144], P(('sect', 'exp'), 'tp'), may hold values from -0.0625 to 0.0625
Outputs:
- mixture: bfloat16 [1024, 6144], P(('sect', 'exp', 'tp'))
Inputs may be any that keep to these rules, and one draw needn't show every extreme that they name: `expert_ids`: each token names two different experts. Among the 8 tokens of one device no expert is named more than 4 times, and in every draw some expert is named exactly 4 times by the tokens of some device.
All inputs are finite; a program needn't handle non-finite values.
Results may differ from a plain program's by a relative error of at most 0.0049.
Values may be sent and summed in bfloat16 or wider, within the bound.
A program may use at most 128 MiB of HBM per device.

v0:
```python
import jax
import jax.numpy as jnp
from jax import lax
from jax.sharding import PartitionSpec as P


def place_slots(ids_block, experts):
    flat_ids = ids_block.reshape(-1)
    hits_mask = (flat_ids[:, None] == jnp.arange(experts, dtype=jnp.int32)[None, :]).astype(
        jnp.int32
    )
    earlier = jnp.cumsum(hits_mask, axis=0) - hits_mask
    slot_rank = jnp.sum(earlier * hits_mask, axis=1)
    return (flat_ids, slot_rank)


def per_device(tokens, router_logits, expert_ids, w_gate, w_up, w_down):
    device_count = lax.axis_size(("sect", "exp", "tp"))
    tp_count = lax.axis_size("tp")
    experts_all = device_count // tp_count // 4
    token_count = tokens.shape[0]
    capacity = min(token_count, 4 * token_count // experts_all)
    model_width = tokens.shape[1]
    quarter_width = model_width // tp_count
    flat_ids, slot_rank = place_slots(expert_ids, experts_all)
    columns = flat_ids * capacity + slot_rank
    positions = jnp.arange(experts_all * capacity, dtype=jnp.int32)
    picker = (positions[:, None] == columns[None, :]).astype(jnp.bfloat16)
    repeated = jnp.repeat(tokens, 2, axis=0)
    slab_rows = jnp.dot(picker, repeated, preferred_element_type=jnp.float32).astype(jnp.bfloat16)
    slab_rows = slab_rows.reshape(experts_all, capacity, model_width)
    fanout = device_count // experts_all
    outbound = jnp.repeat(slab_rows, fanout, axis=0)
    received = lax.all_to_all(
        outbound, ("sect", "exp", "tp"), split_axis=0, concat_axis=0, tiled=True
    )
    row_count = device_count * capacity
    expert_rows = received.reshape(row_count, model_width)
    gate_proj = jnp.dot(expert_rows, w_gate[0], preferred_element_type=jnp.float32)
    up_proj = jnp.dot(expert_rows, w_up[0], preferred_element_type=jnp.float32)
    hidden = (jax.nn.silu(gate_proj) * up_proj).astype(jnp.bfloat16)
    partial_value = jnp.dot(hidden, w_down[0], preferred_element_type=jnp.float32)
    owned_part = lax.psum_scatter(partial_value, "tp", scatter_dimension=1, tiled=True)
    returned = lax.all_to_all(
        owned_part.reshape(device_count, capacity, quarter_width),
        ("sect", "exp", "tp"),
        split_axis=0,
        concat_axis=0,
        tiled=True,
    )
    piece_sums = jnp.sum(
        returned.reshape(experts_all, 4, tp_count, capacity, quarter_width), axis=1
    )
    expert_out = piece_sums.transpose(0, 2, 1, 3).reshape(experts_all * capacity, model_width)
    weights = jax.nn.sigmoid(router_logits - router_logits[:, ::-1]).reshape(-1)
    combine_w = jnp.where(positions[None, :] == columns[:, None], weights[:, None], 0.0)
    combine_w = jnp.sum(combine_w.reshape(token_count, 2, experts_all * capacity), axis=1)
    mixture = jnp.dot(
        combine_w, expert_out, precision=lax.Precision.HIGHEST, preferred_element_type=jnp.float32
    )
    return mixture.astype(jnp.bfloat16)


def solution(mesh):
    in_specs = (
        P(("sect", "exp", "tp"), None),
        P(("sect", "exp", "tp"), None),
        P(("sect", "exp", "tp"), None),
        P(("sect", "exp"), None, "tp"),
        P(("sect", "exp"), None, "tp"),
        P(("sect", "exp"), "tp", None),
    )
    out_specs = P(("sect", "exp", "tp"), None)
    return jax.shard_map(
        per_device, mesh=mesh, in_specs=in_specs, out_specs=out_specs, check_vma=False
    )
```

profile of v0, /device:TPU:1, one launch (start us, length us, event | category | flops | bytes accessed | tf_op | source)
XLA Modules:
  0.0 310.4 jit_solution(16165600053906580294)
XLA Ops:
  6.5 0.0 reduce-scatter.2.cloned.1.call-start
  6.5 0.8 copy.17
  7.3 0.1 eq.43
  7.4 0.1 fusion.13
  7.5 0.2 select_reduce_fusion.1
  7.7 1.0 broadcast_in_dim.25
  8.7 0.1 reshape.54
  8.8 0.2 convolution_convert_fusion
  9.0 0.1 reshape.55
  9.2 3.1 %broadcast_in_dim.26 = bf16[8,16,4,6144]{3,2,1,0:T(4,128)(2,1)S(1)} broadcast(bf16[8,4,6144]{2,1,0:T(4,128)(2,1)S(1)} %reshape.55), dimensions={0,2,3} | broadcast | bytes 6684672 | tf_op jit(solution)/shard_map/broadcast_in_dim | solution.py:33
  12.3 86.0 %all_to_all.10 = bf16[128,4,6144]{2,1,0:T(4,128)(2,1)} all-to-all(bf16[128,4,6144]{2,1,0:T(4,128)(2,1)S(1)} %bitcast.25), channel_id=1, replica_groups=mesh['sect'=2,'exp'=16,'tp'=4] {'sect','exp','tp'}, dimensions={0} | all-to-all | bytes 12582912 | tf_op jit(solution)/shard_map/all_to_all | solution.py:34
  98.3 0.0 slice-start.2
  98.3 10.6 %reshape.57 = bf16[512,6144]{1,0:T(8,128)(2,1)} reshape(bf16[128,4,6144]{2,1,0:T(4,128)(2,1)} %all_to_all.10) | data formatting | bytes 12582912 | tf_op jit(solution)/shard_map/reshape | solution.py:38
  108.9 0.0 copy-start
  108.9 0.0 slice-start.3
  108.9 0.0 slice-start
  108.9 7.6 %fusion.4 = f32[512,512]{1,0:T(8,128)S(1)} fusion(bf16[512,6144]{1,0:T(8,128)(2,1)} %reshape.57, bf16[1,6144,512]{2,1,0:T(8,128)(2,1)} %param.9), kind=kOutput, calls=%fused_computation.6 | convolution fusion | flops 3221225472 | bytes 13631488 | tf_op jit(solution)/shard_map/dot_general | solution.py:39
  116.5 0.0 slice-done.2
  116.5 0.0 copy-done
  116.5 0.0 slice-done.3
  116.5 0.0 slice-start.1
  116.5 3.5 %fusion.9 = bf16[512,512]{1,0:T(8,128)(2,1)S(1)} fusion(bf16[512,6144]{1,0:T(8,128)(2,1)S(1)} %copy-done, bf16[1,6144,512]{2,1,0:T(8,128)(2,1)S(1)} %bitcast.33, f32[512,512]{1,0:T(8,128)S(1)} %fusion.4), kind=kOutput, calls=%fused_computation.9 | convolution fusion | flops 3222798336 | bytes 14155776 | tf_op jit(solution)/shard_map/dot_general | solution.py:40
  120.1 0.0 slice-done
  120.1 0.0 slice-done.1
  120.1 6.4 %fusion = f32[512,6144]{1,0:T(8,128)} fusion(bf16[512,512]{1,0:T(8,128)(2,1)S(1)} %fusion.9, bf16[1,512,6144]{2,1,0:T(8,128)(2,1)S(1)} %bitcast.27), kind=kOutput, calls=%fused_computation.2 | convolution fusion | flops 3221225472 | bytes 19398656 | tf_op jit(solution)/shard_map/dot_general | solution.py:42
  126.5 0.0 reduce-scatter.2.cloned.1.call-update
  126.5 0.0 copy-start.1
  126.5 119.9 %reduce-scatter.2.cloned.1.call-done = f32[512,1536]{1,0:T(8,128)} async-done(((f32[512,6144]{1,0:T(8,128)}), f32[512,1536]{1,0:T(8,128)}) %reduce-scatter.2.cloned.1.call-update) | async-done | bytes 3145744 | tf_op jit(solution)/shard_map/reduce_scatter | solution.py:43
  246.4 4.8 %reshape.58 = f32[128,4,1536]{2,1,0:T(4,128)} reshape(f32[512,1536]{1,0:T(8,128)} %reduce-scatter.2.cloned.1.call-done) | data formatting | bytes 6291456 | tf_op jit(solution)/shard_map/reshape | solution.py:45
  251.2 7.8 %all-to-all-start.1 = ((f32[128,4,1536]{2,1,0:T(4,128)}), f32[128,4,1536]{2,1,0:T(4,128)S(1)}, u32[]{:S(2)}, u32[]{:S(2)}) async-start(f32[128,4,1536]{2,1,0:T(4,128)} %reshape.58), calls=%async_computation.2 | async-start | bytes 6291456 | tf_op jit(solution)/shard_map/all_to_all | solution.py:44
  259.1 0.1 reduce_sum.30
  259.1 0.0 copy-done.1
  259.2 0.1 copy.19
  259.3 0.1 select_reduce_fusion
  259.3 39.5 %all-to-all-done.1 = f32[128,4,1536]{2,1,0:T(4,128)S(1)} async-done(((f32[128,4,1536]{2,1,0:T(4,128)}), f32[128,4,1536]{2,1,0:T(4,128)S(1)}, u32[]{:S(2)}, u32[]{:S(2)}) %all-to-all-start.1) | async-done | bytes 3145760 | tf_op jit(solution)/shard_map/all_to_all | solution.py:44
  298.8 1.9 reduce_sum.32
  300.7 1.4 copy.20
  302.1 0.2 copy.21
  302.4 1.1 convolution_convert_fusion.1
  (7 shorter events, 0.1 us)
Async XLA Ops:
  6.5 239.9 %reduce-scatter.2.cloned.1.call-start = ((), (), s32[]{:S(2)}) async-start(), calls=%async_computation.3 | async-start | bytes 15728640 | tf_op jit(solution)/shard_map/reduce_scatter | solution.py:43
  98.3 18.2 %slice-start.2 = ((s8[6291456]{0:T(1024)(128)(4,1)}), s8[2097152]{0:T(1024)(128)(4,1)S(1)}, s32[]{:S(2)}) async-start(s8[6291456]{0:T(1024)(128)(4,1)} %bitcast.32), calls=%async_computation.6 | async-start | bytes 4194304
  108.9 7.6 %copy-start = (bf16[512,6144]{1,0:T(8,128)(2,1)S(1)}, bf16[512,6144]{1,0:T(8,128)(2,1)}, u32[]{:S(2)}) copy-start(bf16[512,6144]{1,0:T(8,128)(2,1)} %reshape.57) | copy-start | bytes 18874372
  108.9 7.6 %slice-start.3 = ((s8[6291456]{0:T(1024)(128)(4,1)}), s8[4194304]{0:T(1024)(128)(4,1)S(1)}, s32[]{:S(2)}) async-start(s8[6291456]{0:T(1024)(128)(4,1)} %bitcast.32), calls=%async_computation.7 | async-start | bytes 8388608
  108.9 11.2 %slice-start = ((s8[6291456]{0:T(1024)(128)(4,1)}), s8[4194304]{0:T(1024)(128)(4,1)S(1)}, s32[]{:S(2)}) async-start(s8[6291456]{0:T(1024)(128)(4,1)} %bitcast.26), calls=%async_computation.4 | async-start | bytes 8388608
  116.5 3.6 %slice-start.1 = ((s8[6291456]{0:T(1024)(128)(4,1)}), s8[2097152]{0:T(1024)(128)(4,1)S(1)}, s32[]{:S(2)}) async-start(s8[6291456]{0:T(1024)(128)(4,1)} %bitcast.26), calls=%async_computation.5 | async-start | bytes 4194304
  126.5 132.6 %copy-start.1 = (f32[8,2]{0,1:T(2,128)S(1)}, f32[8,2]{0,1:T(2,128)}, u32[]{:S(2)}) copy-start(f32[8,2]{0,1:T(2,128)} %param.7) | copy-start | bytes 196
  251.2 47.6 %all-to-all-start.1 = ((f32[128,4,1536]{2,1,0:T(4,128)}), f32[128,4,1536]{2,1,0:T(4,128)S(1)}, u32[]{:S(2)}, u32[]{:S(2)}) async-start(f32[128,4,1536]{2,1,0:T(4,128)} %reshape.58), calls=%async_computation.2 | async-start | bytes 6291456 | tf_op jit(solution)/shard_map/all_to_all | solution.py:44
Sparse Core Ops, SparseCore 0:
  126.6 119.7 reduce-scatter.1
where the time goes:
time: 313 us; the launch traced here: 310 us
  waiting for transfers between devices  159 us (51%)
  blocking collectives  86 us (27%)
  local copies, waits for them, and re-layouts  22.5 us (7%)
  matrix products  18.9 us (6%)
  between operations  13.5 us (4%)
  starting transfers between devices  7.83 us (3%)
    reduce_scatter x1, waiting for transfers between devices, per_device(): lax.psum_scatter(partial_value, 'tp', scatter_dimension=1, tiled=True)  120 us
    all_to_all x1, blocking collectives, per_device(): lax.all_to_all(outbound, ('sect', 'exp', 'tp'), split_axis=0, concat_axis...  86 us
    all_to_all x1, waiting for transfers between devices, per_device(): lax.all_to_all(owned_part.reshape(device_count, capacity, quarter_width),...  39.5 us
    reshape x1, local copies, waits for them, and re-layouts, per_device(): expert_rows = received.reshape(row_count, model_width)  10.6 us
    all_to_all x1, starting transfers between devices, per_device(): lax.all_to_all(owned_part.reshape(device_count, capacity, quarter_width),...  7.83 us
    dot_general x1, matrix products, per_device(): jnp.dot(expert_rows, w_gate[0], preferred_element_type=jnp.float32)  7.59 us
    dot_general x1, matrix products, per_device(): jnp.dot(hidden, w_down[0], preferred_element_type=jnp.float32)  6.39 us
  transfers between devices with their start and end apart: 2, of which 2 were waited for; matrix products, arithmetic and copies ran while one was open for 0% of the time, Pallas kernels for 0%

commit v1 on v0

v1 whole, which is shorter than its diff:
```python
import jax
import jax.numpy as jnp
import numpy as np
from jax import lax
from jax.sharding import Mesh
from jax.sharding import PartitionSpec as P

ALL = ("sect", "ey", "ex", "tp")
EXPERT_AXES = ("sect", "ey")
PLANE_AXES = ("ex", "tp")


def place_slots(ids_block, experts):
    flat_ids = ids_block.reshape(-1)
    hits_mask = (flat_ids[:, None] == jnp.arange(experts, dtype=jnp.int32)[None, :]).astype(
        jnp.int32
    )
    earlier = jnp.cumsum(hits_mask, axis=0) - hits_mask
    slot_rank = jnp.sum(earlier * hits_mask, axis=1)
    return (flat_ids, slot_rank)


def per_device(tokens, router_logits, expert_ids, w_gate, w_up, w_down):
    experts_all = lax.axis_size(EXPERT_AXES)
    plane_count = lax.axis_size(PLANE_AXES)
    token_count = tokens.shape[0]
    capacity = min(token_count, 4 * token_count // experts_all)
    model_width = tokens.shape[1]
    flat_ids, slot_rank = place_slots(expert_ids, experts_all)
    columns = flat_ids * capacity + slot_rank
    positions = jnp.arange(experts_all * capacity, dtype=jnp.int32)
    picker = (positions[:, None] == columns[None, :]).astype(jnp.bfloat16)
    repeated = jnp.repeat(tokens, 2, axis=0)
    slab = jnp.dot(picker, repeated, preferred_element_type=jnp.float32).astype(jnp.bfloat16)
    slab = slab.reshape(experts_all, capacity, model_width)
    column_rows = lax.all_to_all(slab, EXPERT_AXES, split_axis=0, concat_axis=0, tiled=True)
    plane_rows = lax.all_gather(column_rows, PLANE_AXES, axis=0, tiled=False)
    row_count = plane_count * experts_all * capacity
    expert_rows = plane_rows.reshape(row_count, model_width)
    gate_proj = jnp.dot(expert_rows, w_gate[0], preferred_element_type=jnp.float32)
    up_proj = jnp.dot(expert_rows, w_up[0], preferred_element_type=jnp.float32)
    hidden = (jax.nn.silu(gate_proj) * up_proj).astype(jnp.bfloat16)
    partial_value = jnp.dot(hidden, w_down[0], preferred_element_type=jnp.float32)
    partial_value = partial_value.reshape(plane_count, experts_all * capacity, model_width)
    owned = lax.psum_scatter(partial_value, PLANE_AXES, scatter_dimension=0, tiled=True)
    owned = owned.reshape(experts_all, capacity, model_width)
    returned = lax.all_to_all(owned, EXPERT_AXES, split_axis=0, concat_axis=0, tiled=True)
    expert_out = returned.reshape(experts_all * capacity, model_width)
    weights = jax.nn.sigmoid(router_logits - router_logits[:, ::-1]).reshape(-1)
    picked = jnp.take(expert_out, columns, axis=0) * weights[:, None]
    mixture = jnp.sum(picked.reshape(token_count, 2, model_width), axis=1)
    return mixture.astype(jnp.bfloat16)


def x_extent(devices):
    coords = [getattr(d, "coords", None) for d in devices.flat]
    if all(c is not None for c in coords):
        return len({c[0] for c in coords})
    return int(round(np.sqrt(devices.shape[1])))


def solution(mesh):
    devices = mesh.devices
    sect, exp, tp = devices.shape
    ex = x_extent(devices)
    fine = Mesh(devices.reshape(sect, exp // ex, ex, tp), ALL)
    in_specs = (
        P(ALL, None),
        P(ALL, None),
        P(ALL, None),
        P(EXPERT_AXES + PLANE_AXES[:1], None, "tp"),
        P(EXPERT_AXES + PLANE_AXES[:1], None, "tp"),
        P(EXPERT_AXES + PLANE_AXES[:1], "tp", None),
    )
    out_specs = P(ALL, None)
    return jax.shard_map(
        per_device, mesh=fine, in_specs=in_specs, out_specs=out_specs, check_vma=False
    )
```

time: 313 us -> 237 us (0.76)
  blocking collectives: 86 us -> 13.9 us
  waiting for transfers between devices: 159 us -> 168 us
  local copies, waits for them, and re-layouts: 22.5 us -> 16.9 us
    reduce_scatter x1 -> x0, waiting for transfers between devices: 120 us -> none  [per_device(): lax.psum_scatter(partial_value, 'tp', scatter_dimension=1, tiled=True)]
    unnamed x1 -> x3, waiting for transfers between devices: 0.02 us -> 93.7 us
    all_to_all x1, blocking collectives: 86 us -> 13.9 us  [per_device(): lax.all_to_all(slab, EXPERT_AXES, split_axis=0, concat_axis=0, tiled=True)]
    all_gather x0 -> x1, waiting for transfers between devices: none -> 62.2 us  [per_device(): plane_rows = lax.all_gather(column_rows, PLANE_AXES, axis=0, tiled=False)]
    all_to_all x1, waiting for transfers between devices: 39.5 us -> 12 us  [per_device(): lax.all_to_all(owned, EXPERT_AXES, split_axis=0, concat_axis=0, tiled=True)]
    reshape x3 -> x5, local copies, waits for them, and re-layouts: 15.5 us -> 13.4 us  [the longest x1 10.6 us: per_device(): expert_rows = plane_rows.reshape(row_count, model_width)]
  transfers between devices with their start and end apart: 2 -> 3, of which waited for: 2 -> 3; matrix products, arithmetic and copies ran while one was open for 0% -> 0% of each run, Pallas kernels for 0% -> 0%
where the time goes in v1:
time: 237 us
  waiting for transfers between devices  168 us (71%)
  matrix products  17.6 us (7%)
  local copies, waits for them, and re-layouts  16.9 us (7%)
  blocking collectives  13.9 us (6%)
  between operations  13.5 us (6%)
  starting transfers between devices  5.17 us (2%)
    unnamed x3, waiting for transfers between devices  93.7 us
    all_gather x1, waiting for transfers between devices, per_device(): plane_rows = lax.all_gather(column_rows, PLANE_AXES, axis=0, tiled=False)  62.2 us
    all_to_all x1, blocking collectives, per_device(): lax.all_to_all(slab, EXPERT_AXES, split_axis=0, concat_axis=0, tiled=True)  13.9 us
    all_to_all x1, waiting for transfers between devices, per_device(): lax.all_to_all(owned, EXPERT_AXES, split_axis=0, concat_axis=0, tiled=True)  12 us
    reshape x1, local copies, waits for them, and re-layouts, per_device(): expert_rows = plane_rows.reshape(row_count, model_width)  10.6 us
    dot_general x1, matrix products, per_device(): jnp.dot(expert_rows, w_gate[0], preferred_element_type=jnp.float32)  7.59 us
    dot_general x1, matrix products, per_device(): jnp.dot(hidden, w_down[0], preferred_element_type=jnp.float32)  6.32 us
    all_to_all x1, starting transfers between devices, per_device(): lax.all_to_all(owned, EXPERT_AXES, split_axis=0, concat_axis=0, tiled=True)  5.13 us
  transfers between devices with their start and end apart: 3, of which 3 were waited for; matrix products, arithmetic and copies ran while one was open for 0% of the time, Pallas kernels for 0%

profile of v1, /device:TPU:1, one launch (start us, length us, event | category | flops | bytes accessed | tf_op | source)
XLA Modules:
  0.0 236.6 jit_solution(15759719655129442192)
XLA Ops:
  6.5 0.0 all-gather.3.cloned.1.call-start
  6.5 0.8 copy.13
  7.3 0.1 reshape.77
  7.4 0.1 fusion.13
  7.5 0.2 select_reduce_fusion
  7.7 1.0 broadcast_in_dim.17
  8.7 0.1 reshape.78
  8.8 0.2 convolution_convert_fusion
  9.0 0.1 reshape.79
  9.2 13.9 %all_to_all.10 = bf16[8,4,6144]{2,1,0:T(4,128)(2,1)} all-to-all(bf16[8,4,6144]{2,1,0:T(4,128)(2,1)S(1)} %reshape.79), channel_id=1, replica_groups=mesh['sect'=2,'ey'=4,'ex'=4,'tp'=4] {'sect','ey'}, dimensions={0} | all-to-all | bytes 786432 | tf_op jit(solution)/shard_map/all_to_all | solution.py:36
  23.0 0.0 all-gather.3.cloned.1.call-update
  23.0 0.0 reduce-scatter.4.cloned.1.call-start
  23.1 62.2 %all-gather.3.cloned.1.call-done = bf16[128,4,6144]{2,1,0:T(4,128)(2,1)} async-done(((bf16[8,4,6144]{2,1,0:T(4,128)(2,1)}), bf16[128,4,6144]{2,1,0:T(4,128)(2,1)}) %all-gather.3.cloned.1.call-update) | async-done | bytes 6291472 | tf_op jit(solution)/shard_map/all_gather | solution.py:37
  85.3 0.0 slice-start
  85.3 10.6 %reshape.80 = bf16[512,6144]{1,0:T(8,128)(2,1)} reshape(bf16[128,4,6144]{2,1,0:T(4,128)(2,1)} %all-gather.3.cloned.1.call-done) | data formatting | bytes 12582912 | tf_op jit(solution)/shard_map/reshape | solution.py:39
  95.9 0.0 copy-start
  95.9 0.0 slice-start.1
  95.9 0.0 slice-start.2
  95.9 7.6 %fusion.4 = f32[512,512]{1,0:T(8,128)S(1)} fusion(bf16[512,6144]{1,0:T(8,128)(2,1)} %reshape.80, bf16[1,6144,512]{2,1,0:T(8,128)(2,1)} %param.9), kind=kOutput, calls=%fused_computation.6 | convolution fusion | flops 3221225472 | bytes 13631488 | tf_op jit(solution)/shard_map/dot_general | solution.py:40
  103.5 0.0 slice-done
  103.5 0.0 copy-done
  103.5 0.0 slice-done.1
  103.5 0.0 slice-start.3
  103.5 3.5 %fusion.9 = bf16[512,512]{1,0:T(8,128)(2,1)S(1)} fusion(bf16[512,6144]{1,0:T(8,128)(2,1)S(1)} %copy-done, bf16[1,6144,512]{2,1,0:T(8,128)(2,1)S(1)} %bitcast.27, f32[512,512]{1,0:T(8,128)S(1)} %fusion.4), kind=kOutput, calls=%fused_computation.9 | convolution fusion | flops 3222798336 | bytes 14155776 | tf_op jit(solution)/shard_map/dot_general | solution.py:41
  107.0 0.0 slice-done.2
  107.0 0.0 slice-done.3
  107.0 6.3 %fusion = f32[16,32,6144]{2,1,0:T(8,128)} fusion(bf16[16,32,512]{2,1,0:T(8,128)(2,1)S(1)} %bitcast.30, bf16[1,512,6144]{2,1,0:T(8,128)(2,1)S(1)} %bitcast.29), kind=kOutput, calls=%fused_computation.2 | convolution fusion | flops 3221225472 | bytes 19398656 | tf_op jit(solution)/shard_map/dot_general | solution.py:43
  113.4 0.0 copy-start.1
  113.4 0.0 reduce-scatter.4.cloned.1.call-update
  113.4 0.1 reduce_sum.23
  113.5 0.1 mul.46
  113.6 0.5 copy-done.1
  114.1 93.7 %reduce-scatter.4.cloned.1.call-done = f32[1,32,6144]{2,1,0:T(8,128)} async-done(((f32[16,32,6144]{2,1,0:T(8,128)}), f32[1,32,6144]{2,1,0:T(8,128)}) %reduce-scatter.4.cloned.1.call-update) | async-done | bytes 786448
  207.7 2.2 reshape.81
  210.0 5.1 %all-to-all-start.1 = ((f32[8,4,6144]{2,1,0:T(4,128)}), f32[8,4,6144]{2,1,0:T(4,128)S(1)}, u32[]{:S(2)}, u32[]{:S(2)}) async-start(f32[8,4,6144]{2,1,0:T(4,128)} %reshape.81), calls=%async_computation.1 | async-start | bytes 1572864 | tf_op jit(solution)/shard_map/all_to_all | solution.py:47
  215.1 0.1 copy.15
  215.2 12.0 %all-to-all-done.1 = f32[8,4,6144]{2,1,0:T(4,128)S(1)} async-done(((f32[8,4,6144]{2,1,0:T(4,128)}), f32[8,4,6144]{2,1,0:T(4,128)S(1)}, u32[]{:S(2)}, u32[]{:S(2)}) %all-to-all-start.1) | async-done | bytes 786464 | tf_op jit(solution)/shard_map/all_to_all | solution.py:47
  227.3 0.3 reshape.82
  227.6 0.7 gather_fusion
  228.2 0.2 gather.7
  228.5 1.2 multiply_reduce_fusion
  (10 shorter events, 0.1 us)
Async XLA Ops:
  6.5 78.7 %all-gather.3.cloned.1.call-start = ((), (), s32[]{:S(2)}) async-start(), calls=%async_computation.3 | async-start | bytes 6684672 | tf_op jit(solution)/shard_map/all_gather | solution.py:37
  23.0 184.7 %reduce-scatter.4.cloned.1.call-start = ((), (), s32[]{:S(2)}) async-start(), calls=%async_computation.4 | async-start | bytes 13369344
  85.3 18.2 %slice-start = ((s8[6291456]{0:T(1024)(128)(4,1)}), s8[2097152]{0:T(1024)(128)(4,1)S(1)}, s32[]{:S(2)}) async-start(s8[6291456]{0:T(1024)(128)(4,1)} %bitcast.26), calls=%async_computation.5 | async-start | bytes 4194304
  95.9 7.6 %copy-start = (bf16[512,6144]{1,0:T(8,128)(2,1)S(1)}, bf16[512,6144]{1,0:T(8,128)(2,1)}, u32[]{:S(2)}) copy-start(bf16[512,6144]{1,0:T(8,128)(2,1)} %reshape.80) | copy-start | bytes 18874372
  95.9 7.6 %slice-start.1 = ((s8[6291456]{0:T(1024)(128)(4,1)}), s8[4194304]{0:T(1024)(128)(4,1)S(1)}, s32[]{:S(2)}) async-start(s8[6291456]{0:T(1024)(128)(4,1)} %bitcast.26), calls=%async_computation.6 | async-start | bytes 8388608
  95.9 11.2 %slice-start.2 = ((s8[6291456]{0:T(1024)(128)(4,1)}), s8[4194304]{0:T(1024)(128)(4,1)S(1)}, s32[]{:S(2)}) async-start(s8[6291456]{0:T(1024)(128)(4,1)} %bitcast.28), calls=%async_computation.7 | async-start | bytes 8388608
  103.5 3.5 %slice-start.3 = ((s8[6291456]{0:T(1024)(128)(4,1)}), s8[2097152]{0:T(1024)(128)(4,1)S(1)}, s32[]{:S(2)}) async-start(s8[6291456]{0:T(1024)(128)(4,1)} %bitcast.28), calls=%async_computation.8 | async-start | bytes 4194304
  113.4 0.7 copy-start.1
  210.0 17.3 %all-to-all-start.1 = ((f32[8,4,6144]{2,1,0:T(4,128)}), f32[8,4,6144]{2,1,0:T(4,128)S(1)}, u32[]{:S(2)}, u32[]{:S(2)}) async-start(f32[8,4,6144]{2,1,0:T(4,128)} %reshape.81), calls=%async_computation.1 | async-start | bytes 1572864 | tf_op jit(solution)/shard_map/all_to_all | solution.py:47
Sparse Core Ops, SparseCore 0:
  23.2 62.0 all-gather.2
  113.5 94.1 reduce-scatter.3

commit v2 on v1

--- a/solution.py
+++ b/solution.py
@@ -2,8 +2,150 @@
 import jax.numpy as jnp
 import numpy as np
 from jax import lax
+from jax.experimental import pallas as pl
+from jax.experimental.pallas import tpu as pltpu
 from jax.sharding import Mesh
 from jax.sharding import PartitionSpec as P
+
+MESH_ID = pl.DeviceIdType.MESH
+
+
+def rs_kernel(p_ref, out_ref, s1, s2, send1, recv1, send2, recv2):
+    nx, nz, rows, width = p_ref.shape
+    quarter = width // 4
+    c = lax.axis_index("sect")
+    y = lax.axis_index("ey")
+    mx = lax.axis_index("ex")
+    mz = lax.axis_index("tp")
+
+    def dev(axis, d):
+        if axis == "z":
+            return (c, y, mx, lax.rem(mz + d + nz, nz))
+        return (c, y, lax.rem(mx + d + nx, nx), mz)
+
+    barrier = pltpu.get_barrier_semaphore()
+    for axis in ("x", "z"):
+        for d in (1, -1):
+            pl.semaphore_signal(barrier, inc=1, device_id=dev(axis, d), device_id_type=MESH_ID)
+    pl.semaphore_wait(barrier, 4)
+
+    rings = [("z", 1), ("z", -1), ("x", 1), ("x", -1)]
+
+    def me_on(axis):
+        return mz if axis == "z" else mx
+
+    def size_on(axis):
+        return nz if axis == "z" else nx
+
+    def cols(r):
+        return pl.ds(r * quarter, quarter)
+
+    def own1(r, j):
+        if rings[r][0] == "z":
+            return p_ref.at[:, j, :, cols(r)]
+        return p_ref.at[j, :, :, cols(r)]
+
+    def own2(r, i):
+        return s1.at[r, size_on(rings[r][0]) - 2, i]
+
+    def other(axis):
+        return "x" if axis == "z" else "z"
+
+    def run_phase(axis_of, own, slots, send, recv, lead):
+        copies = {}
+        n = size_on(axis_of(0))
+        for s in range(n - 1):
+            for r in range(4):
+                axis, d = axis_of(r), rings[r][1]
+                me = me_on(axis)
+                j = lax.rem(me + n * (s + 2) - d * (s + 1), n)
+                if s == 0:
+                    src = own(r, j)
+                else:
+                    copies[(r, s - 1)].wait_recv()
+                    for t in range(lead):
+                        slots[r, s - 1, t] += own(r, j)[t]
+                    src = slots.at[r, s - 1]
+                cp = pltpu.make_async_remote_copy(
+                    src_ref=src,
+                    dst_ref=slots.at[r, s],
+                    send_sem=send.at[r, s],
+                    recv_sem=recv.at[r, s],
+                    device_id=dev(axis, d),
+                    device_id_type=MESH_ID,
+                )
+                cp.start()
+                copies[(r, s)] = cp
+        return copies, n
+
+    def add_own(slot_ref, own_ref, lead):
+        for t in range(lead):
+            slot_ref[t] += own_ref[t]
+
+    copies1, n1 = run_phase(lambda r: rings[r][0], own1, s1, send1, recv1, 4)
+    for r in range(4):
+        copies1[(r, n1 - 2)].wait_recv()
+        axis = rings[r][0]
+        add_own(s1.at[r, n1 - 2], own1(r, me_on(axis)), 4)
+
+    def own2b(r, i):
+        return s1.at[r, n1 - 2, i]
+
+    def run_phase2():
+        copies = {}
+        n = 4
+        for s in range(n - 1):
+            for r in range(4):
+                axis, d = other(rings[r][0]), rings[r][1]
+                me = me_on(axis)
+                j = lax.rem(me + n * (s + 2) - d * (s + 1), n)
+                if s == 0:
+                    src = own2b(r, j)
+                else:
+                    copies[(r, s - 1)].wait_recv()
+                    s2[r, s - 1] += own2b(r, j)[...]
+                    src = s2.at[r, s - 1]
+                cp = pltpu.make_async_remote_copy(
+                    src_ref=src,
+                    dst_ref=s2.at[r, s],
+                    send_sem=send2.at[r, s],
+                    recv_sem=recv2.at[r, s],
+                    device_id=dev(axis, d),
+                    device_id_type=MESH_ID,
+                )
+                cp.start()
+                copies[(r, s)] = cp
+        return copies, n
+
+    copies2, n2 = run_phase2()
+    for r in range(4):
+        copies2[(r, n2 - 2)].wait_recv()
+        axis = other(rings[r][0])
+        out_ref[:, cols(r)] = s2[r, n2 - 2] + own2b(r, me_on(axis))[...]
+    for cp in list(copies1.values()) + list(copies2.values()):
+        cp.wait_send()
+
+
+def plane_reduce_scatter(partial):
+    nx, nz, rows, width = partial.shape
+    quarter = width // 4
+    return pl.pallas_call(
+        rs_kernel,
+        out_shape=jax.ShapeDtypeStruct((rows, width), jnp.float32),
+        in_specs=[pl.BlockSpec(memory_space=pltpu.VMEM)],
+        out_specs=pl.BlockSpec(memory_space=pltpu.VMEM),
+        scratch_shapes=[
+            pltpu.VMEM((4, nz - 1, nx, rows, quarter), jnp.float32),
+            pltpu.VMEM((4, nx - 1, rows, quarter), jnp.float32),
+            pltpu.SemaphoreType.DMA((4, nz - 1)),
+            pltpu.SemaphoreType.DMA((4, nz - 1)),
+            pltpu.SemaphoreType.DMA((4, nx - 1)),
+            pltpu.SemaphoreType.DMA((4, nx - 1)),
+        ],
+        compiler_params=pltpu.CompilerParams(
+            collective_id=0, has_side_effects=True, vmem_limit_bytes=60 * 1024 * 1024
+        ),
+    )(partial)
 
 ALL = ("sect", "ey", "ex", "tp")
 EXPERT_AXES = ("sect", "ey")
@@ -41,8 +183,11 @@
     up_proj = jnp.dot(expert_rows, w_up[0], preferred_element_type=jnp.float32)
     hidden = (jax.nn.silu(gate_proj) * up_proj).astype(jnp.bfloat16)
     partial_value = jnp.dot(hidden, w_down[0], preferred_element_type=jnp.float32)
-    partial_value = partial_value.reshape(plane_count, experts_all * capacity, model_width)
-    owned = lax.psum_scatter(partial_value, PLANE_AXES, scatter_dimension=0, tiled=True)
+    nx = lax.axis_size("ex")
+    partial_value = partial_value.reshape(
+        nx, plane_count // nx, experts_all * capacity, model_width
+    )
+    owned = plane_reduce_scatter(partial_value)
     owned = owned.reshape(experts_all, capacity, model_width)
     returned = lax.all_to_all(owned, EXPERT_AXES, split_axis=0, concat_axis=0, tiled=True)
     expert_out = returned.reshape(experts_all * capacity, model_width)

time: 237 us -> 228 us (0.962)
  waiting for transfers between devices: 168 us -> 73.4 us
  Pallas kernels: 0 us -> 77.3 us
  starting transfers between devices: 5.17 us -> 10.6 us
  matrix products: 17.6 us -> 20.7 us
    unnamed x3 -> x1, waiting for transfers between devices: 93.7 us -> 0.02 us
    pallas_call x0 -> x1, Pallas kernels: none -> 77.3 us  [plane_reduce_scatter(): pl.pallas_call(rs_kernel, out_shape=jax.ShapeDtypeStruct((rows, width), j...]
    all_to_all x1, starting transfers between devices: 5.13 us -> 10.6 us  [per_device(): lax.all_to_all(owned, EXPERT_AXES, split_axis=0, concat_axis=0, tiled=True)]
    dot_general x1, matrix products: 3.49 us -> 6.43 us  [per_device(): up_proj = jnp.dot(expert_rows, w_up[0], preferred_element_type=jnp.float32)]
  transfers between devices with their start and end apart: 3 -> 2, of which waited for: 3 -> 2; matrix products, arithmetic and copies ran while one was open for 0% -> 0% of each run, Pallas kernels for 0% -> 0%
where the time goes in v2:
time: 228 us
  Pallas kernels  77.3 us (34%)
  waiting for transfers between devices  73.4 us (32%)
  matrix products  20.7 us (9%)
  local copies, waits for them, and re-layouts  16.9 us (7%)
  blocking collectives  13.9 us (6%)
  between operations  13.5 us (6%)
  starting transfers between devices  10.6 us (5%)
    pallas_call x1, Pallas kernels, plane_reduce_scatter(): pl.pallas_call(rs_kernel, out_shape=jax.ShapeDtypeStruct((rows, width), j...  77.3 us
    all_gather x1, waiting for transfers between devices, per_device(): plane_rows = lax.all_gather(column_rows, PLANE_AXES, axis=0, tiled=False)  61.3 us
    all_to_all x1, blocking collectives, per_device(): lax.all_to_all(slab, EXPERT_AXES, split_axis=0, concat_axis=0, tiled=True)  13.9 us
    all_to_all x1, waiting for transfers between devices, per_device(): lax.all_to_all(owned, EXPERT_AXES, split_axis=0, concat_axis=0, tiled=True)  12 us
    all_to_all x1, starting transfers between devices, per_device(): lax.all_to_all(owned, EXPERT_AXES, split_axis=0, concat_axis=0, tiled=True)  10.6 us
    reshape x1, local copies, waits for them, and re-layouts, per_device(): expert_rows = plane_rows.reshape(row_count, model_width)  10.4 us
    dot_general x1, matrix products, per_device(): jnp.dot(expert_rows, w_gate[0], preferred_element_type=jnp.float32)  7.58 us
    dot_general x1, matrix products, per_device(): jnp.dot(hidden, w_down[0], preferred_element_type=jnp.float32)  6.47 us
  transfers between devices with their start and end apart: 2, of which 2 were waited for; matrix products, arithmetic and copies ran while one was open for 0% of the time, Pallas kernels for 0%

profile of v2, /device:TPU:1, one launch (start us, length us, event | category | flops | bytes accessed | tf_op | source)
XLA Modules:
  0.0 227.9 jit_solution(7600746575472990018)
XLA Ops:
  6.5 0.0 all-gather.3.cloned.1.call-start
  6.5 0.8 copy.13
  7.3 0.1 reshape.77
  7.4 0.1 fusion.13
  7.5 0.2 select_reduce_fusion
  7.7 1.0 broadcast_in_dim.17
  8.7 0.1 reshape.78
  8.8 0.2 convolution_convert_fusion
  9.0 0.1 reshape.79
  9.2 13.9 %all_to_all.10 = bf16[8,4,6144]{2,1,0:T(4,128)(2,1)} all-to-all(bf16[8,4,6144]{2,1,0:T(4,128)(2,1)S(1)} %reshape.79), channel_id=1, replica_groups=mesh['sect'=2,'ey'=4,'ex'=4,'tp'=4] {'sect','ey'}, dimensions={0} | all-to-all | bytes 786432 | tf_op jit(solution)/shard_map/all_to_all | solution.py:178
  23.0 0.0 all-gather.3.cloned.1.call-update
  23.0 0.1 reduce_sum.23
  23.1 0.1 mul.46
  23.2 0.7 rev.3
  23.9 61.3 %all-gather.3.cloned.1.call-done = bf16[128,4,6144]{2,1,0:T(4,128)(2,1)} async-done(((bf16[8,4,6144]{2,1,0:T(4,128)(2,1)}), bf16[128,4,6144]{2,1,0:T(4,128)(2,1)}) %all-gather.3.cloned.1.call-update) | async-done | bytes 6291472 | tf_op jit(solution)/shard_map/all_gather | solution.py:179
  85.3 10.4 %reshape.80 = bf16[512,6144]{1,0:T(8,128)(2,1)} reshape(bf16[128,4,6144]{2,1,0:T(4,128)(2,1)} %all-gather.3.cloned.1.call-done) | data formatting | bytes 12582912 | tf_op jit(solution)/shard_map/reshape | solution.py:181
  95.7 0.0 copy-start
  95.7 0.0 slice-start
  95.7 7.6 %fusion.4 = f32[512,512]{1,0:T(8,128)S(1)} fusion(bf16[512,6144]{1,0:T(8,128)(2,1)} %reshape.80, bf16[1,6144,512]{2,1,0:T(8,128)(2,1)} %param.9), kind=kOutput, calls=%fused_computation.6 | convolution fusion | flops 3221225472 | bytes 13631488 | tf_op jit(solution)/shard_map/dot_general | solution.py:182
  103.3 0.0 copy-done
  103.3 0.0 slice-start.1
  103.3 6.4 %fusion.9 = bf16[512,512]{1,0:T(8,128)(2,1)S(1)} fusion(bf16[512,6144]{1,0:T(8,128)(2,1)S(1)} %copy-done, bf16[1,6144,512]{2,1,0:T(8,128)(2,1)} %param.10, f32[512,512]{1,0:T(8,128)S(1)} %fusion.4), kind=kOutput, calls=%fused_computation.9 | convolution fusion | flops 3222798336 | bytes 14155776 | tf_op jit(solution)/shard_map/dot_general | solution.py:183
  109.8 0.0 slice-done
  109.8 0.0 slice-done.1
  109.8 6.5 %fusion.p_ref = f32[4,4,32,6144]{3,2,1,0:T(8,128)} fusion(bf16[4,4,32,512]{3,2,1,0:T(8,128)(2,1)S(1)} %bitcast.30, bf16[1,512,6144]{2,1,0:T(8,128)(2,1)S(1)} %bitcast.29), kind=kOutput, calls=%fused_computation.2 | convolution fusion | flops 3221225472 | bytes 19398656 | tf_op jit(solution)/shard_map/dot_general | solution.py:185
  116.2 0.0 copy-start.1
  116.3 77.3 %shard_map.64 = f32[32,6144]{1,0:T(8,128)} custom-call(f32[4,4,32,6144]{3,2,1,0:T(8,128)} %fusion.p_ref), custom_call_target="tpu_custom_call" | custom-call | tf_op jit(solution)/shard_map/pallas_call | solution.py:132
  193.6 2.3 reshape.81
  195.8 10.6 %all-to-all-start.1 = ((f32[8,4,6144]{2,1,0:T(4,128)}), f32[8,4,6144]{2,1,0:T(4,128)S(1)}, u32[]{:S(2)}, u32[]{:S(2)}) async-start(f32[8,4,6144]{2,1,0:T(4,128)} %reshape.81), calls=%async_computation.1 | async-start | bytes 1572864 | tf_op jit(solution)/shard_map/all_to_all | solution.py:192
  206.5 0.0 copy-done.1
  206.5 0.1 copy.15
  206.6 12.0 %all-to-all-done.1 = f32[8,4,6144]{2,1,0:T(4,128)S(1)} async-done(((f32[8,4,6144]{2,1,0:T(4,128)}), f32[8,4,6144]{2,1,0:T(4,128)S(1)}, u32[]{:S(2)}, u32[]{:S(2)}) %all-to-all-start.1) | async-done | bytes 786464 | tf_op jit(solution)/shard_map/all_to_all | solution.py:192
  218.6 0.3 reshape.82
  218.9 0.7 gather_fusion
  219.6 0.2 gather.7
  219.8 1.2 multiply_reduce_fusion
  (8 shorter events, 0.1 us)
Async XLA Ops:
  6.5 78.7 %all-gather.3.cloned.1.call-start = ((), (), s32[]{:S(2)}) async-start(), calls=%async_computation.2 | async-start | bytes 6684672 | tf_op jit(solution)/shard_map/all_gather | solution.py:179
  95.7 7.6 %copy-start = (bf16[512,6144]{1,0:T(8,128)(2,1)S(1)}, bf16[512,6144]{1,0:T(8,128)(2,1)}, u32[]{:S(2)}) copy-start(bf16[512,6144]{1,0:T(8,128)(2,1)} %reshape.80) | copy-start | bytes 18874372
  95.7 14.1 %slice-start = ((s8[6291456]{0:T(1024)(128)(4,1)}), s8[4194304]{0:T(1024)(128)(4,1)S(1)}, s32[]{:S(2)}) async-start(s8[6291456]{0:T(1024)(128)(4,1)} %bitcast.28), calls=%async_computation.3 | async-start | bytes 8388608
  103.3 6.5 %slice-start.1 = ((s8[6291456]{0:T(1024)(128)(4,1)}), s8[2097152]{0:T(1024)(128)(4,1)S(1)}, s32[]{:S(2)}) async-start(s8[6291456]{0:T(1024)(128)(4,1)} %bitcast.28), calls=%async_computation.4 | async-start | bytes 4194304
  116.2 90.2 %copy-start.1 = (f32[8,2]{0,1:T(2,128)S(1)}, f32[8,2]{0,1:T(2,128)}, u32[]{:S(2)}) copy-start(f32[8,2]{0,1:T(2,128)} %param.7) | copy-start | bytes 196
  195.8 22.8 %all-to-all-start.1 = ((f32[8,4,6144]{2,1,0:T(4,128)}), f32[8,4,6144]{2,1,0:T(4,128)S(1)}, u32[]{:S(2)}, u32[]{:S(2)}) async-start(f32[8,4,6144]{2,1,0:T(4,128)} %reshape.81), calls=%async_computation.1 | async-start | bytes 1572864 | tf_op jit(solution)/shard_map/all_to_all | solution.py:192
Sparse Core Ops, SparseCore 0:
  23.2 62.0 all-gather.2

commit v3 on v2

--- a/solution.py
+++ b/solution.py
@@ -147,6 +147,113 @@
         ),
     )(partial)
 
+def ag_kernel(in_ref, out_ref, local_sem, send1, recv1, send2, recv2):
+    nx, nz, rows, width = out_ref.shape
+    quarter = width // 4
+    c = lax.axis_index("sect")
+    y = lax.axis_index("ey")
+    mx = lax.axis_index("ex")
+    mz = lax.axis_index("tp")
+
+    def dev(axis, d):
+        if axis == "z":
+            return (c, y, mx, lax.rem(mz + d + nz, nz))
+        return (c, y, lax.rem(mx + d + nx, nx), mz)
+
+    barrier = pltpu.get_barrier_semaphore()
+    for axis in ("x", "z"):
+        for d in (1, -1):
+            pl.semaphore_signal(barrier, inc=1, device_id=dev(axis, d), device_id_type=MESH_ID)
+    pl.semaphore_wait(barrier, 4)
+
+    local = pltpu.make_async_copy(in_ref, out_ref.at[mx, mz], local_sem)
+    local.start()
+
+    rings = [("z", 1), ("z", -1), ("x", 1), ("x", -1)]
+
+    def cols(r):
+        return pl.ds(r * quarter, quarter)
+
+    def block(axis, r, k):
+        if axis == "z":
+            return out_ref.at[mx, k, :, cols(r)]
+        return out_ref.at[k, mz, :, cols(r)]
+
+    def plane_block(axis, r, k):
+        if axis == "x":
+            return out_ref.at[k, :, :, cols(r)]
+        return out_ref.at[:, k, :, cols(r)]
+
+    def me_on(axis):
+        return mz if axis == "z" else mx
+
+    def ring_phase(axis_of, view, first_src, send, recv, sizes):
+        copies = {}
+        n = sizes
+        for s in range(n - 1):
+            for r in range(4):
+                axis, d = axis_of(r), rings[r][1]
+                me = me_on(axis)
+                k = lax.rem(me + n * (s + 1) - d * s, n)
+                if s == 0:
+                    src = first_src(r)
+                else:
+                    copies[(r, s - 1)].wait_recv()
+                    src = view(axis, r, k)
+                cp = pltpu.make_async_remote_copy(
+                    src_ref=src,
+                    dst_ref=view(axis, r, k),
+                    send_sem=send.at[r, s],
+                    recv_sem=recv.at[r, s],
+                    device_id=dev(axis, d),
+                    device_id_type=MESH_ID,
+                )
+                cp.start()
+                copies[(r, s)] = cp
+        for r in range(4):
+            copies[(r, n - 2)].wait_recv()
+        return copies
+
+    copies1 = ring_phase(
+        lambda r: rings[r][0], block, lambda r: in_ref.at[:, cols(r)], send1, recv1, nz
+    )
+    local.wait()
+
+    def second(r):
+        return "x" if rings[r][0] == "z" else "z"
+
+    copies2 = ring_phase(
+        second,
+        plane_block,
+        lambda r: plane_block(second(r), r, me_on(second(r))),
+        send2,
+        recv2,
+        nx,
+    )
+    for cp in list(copies1.values()) + list(copies2.values()):
+        cp.wait_send()
+
+
+def plane_all_gather(rows_block, nx, nz):
+    rows, width = rows_block.shape
+    return pl.pallas_call(
+        ag_kernel,
+        out_shape=jax.ShapeDtypeStruct((nx, nz, rows, width), rows_block.dtype),
+        in_specs=[pl.BlockSpec(memory_space=pltpu.VMEM)],
+        out_specs=pl.BlockSpec(memory_space=pltpu.VMEM),
+        scratch_shapes=[
+            pltpu.SemaphoreType.DMA(()),
+            pltpu.SemaphoreType.DMA((4, nz - 1)),
+            pltpu.SemaphoreType.DMA((4, nz - 1)),
+            pltpu.SemaphoreType.DMA((4, nx - 1)),
+            pltpu.SemaphoreType.DMA((4, nx - 1)),
+        ],
+        compiler_params=pltpu.CompilerParams(
+            collective_id=1, has_side_effects=True, vmem_limit_bytes=60 * 1024 * 1024
+        ),
+    )(rows_block)
+
+
 ALL = ("sect", "ey", "ex", "tp")
 EXPERT_AXES = ("sect", "ey")
 PLANE_AXES = ("ex", "tp")
@@ -176,14 +283,16 @@
     slab = jnp.dot(picker, repeated, preferred_element_type=jnp.float32).astype(jnp.bfloat16)
     slab = slab.reshape(experts_all, capacity, model_width)
     column_rows = lax.all_to_all(slab, EXPERT_AXES, split_axis=0, concat_axis=0, tiled=True)
-    plane_rows = lax.all_gather(column_rows, PLANE_AXES, axis=0, tiled=False)
+    nx = lax.axis_size("ex")
+    plane_rows = plane_all_gather(
+        column_rows.reshape(experts_all * capacity, model_width), nx, plane_count // nx
+    )
     row_count = plane_count * experts_all * capacity
     expert_rows = plane_rows.reshape(row_count, model_width)
     gate_proj = jnp.dot(expert_rows, w_gate[0], preferred_element_type=jnp.float32)
     up_proj = jnp.dot(expert_rows, w_up[0], preferred_element_type=jnp.float32)
     hidden = (jax.nn.silu(gate_proj) * up_proj).astype(jnp.bfloat16)
     partial_value = jnp.dot(hidden, w_down[0], preferred_element_type=jnp.float32)
-    nx = lax.axis_size("ex")
     partial_value = partial_value.reshape(
         nx, plane_count // nx, experts_all * capacity, model_width
     )

time: 228 us -> 189 us (0.83)
  waiting for transfers between devices: 73.4 us -> 19.1 us
  Pallas kernels: 77.3 us -> 116 us
  blocking collectives: 13.9 us -> 0 us
  between operations: 13.5 us -> 0.15 us
  starting transfers between devices: 10.6 us -> 23 us
  local copies, waits for them, and re-layouts: 16.9 us -> 8.04 us
    all_gather x1 -> x0, waiting for transfers between devices: 61.3 us -> none  [per_device(): plane_rows = lax.all_gather(column_rows, PLANE_AXES, axis=0, tiled=False)]
    pallas_call x0 -> x1, Pallas kernels: none -> 44.3 us  [plane_all_gather(): pl.pallas_call(ag_kernel, out_shape=jax.ShapeDtypeStruct((nx, nz, rows, w...]
    all_to_all x1 -> x0, blocking collectives: 13.9 us -> none  [per_device(): lax.all_to_all(slab, EXPERT_AXES, split_axis=0, concat_axis=0, tiled=True)]
    reshape x1, local copies, waits for them, and re-layouts: 10.4 us -> 0.85 us  [per_device(): column_rows.reshape(experts_all * capacity, model_width)]
    all_to_all x0 -> x1, waiting for transfers between devices: none -> 7.1 us  [per_device(): lax.all_to_all(slab, EXPERT_AXES, split_axis=0, concat_axis=0, tiled=True)]
    all_to_all x1, starting transfers between devices: 10.6 us -> 17 us  [per_device(): lax.all_to_all(owned, EXPERT_AXES, split_axis=0, concat_axis=0, tiled=True)]
    all_to_all x0 -> x1, starting transfers between devices: none -> 5.97 us  [per_device(): lax.all_to_all(slab, EXPERT_AXES, split_axis=0, concat_axis=0, tiled=True)]
    pallas_call x1, Pallas kernels: 77.3 us -> 71.7 us  [plane_reduce_scatter(): pl.pallas_call(rs_kernel, out_shape=jax.ShapeDtypeStruct((rows, width), j...]
  transfers between devices with their start and end apart: 2 -> 2, of which waited for: 2 -> 2; matrix products, arithmetic and copies ran while one was open for 0% -> 1% of each run, Pallas kernels for 0% -> 0%
where the time goes in v3:
time: 189 us; the launch traced here: 188 us
  Pallas kernels  116 us (61%)
  starting transfers between devices  23 us (12%)
  matrix products  20.6 us (11%)
  waiting for transfers between devices  19.1 us (10%)
  local copies, waits for them, and re-layouts  8.04 us (4%)
    pallas_call x1, Pallas kernels, plane_reduce_scatter(): pl.pallas_call(rs_kernel, out_shape=jax.ShapeDtypeStruct((rows, width), j...  71.7 us
    pallas_call x1, Pallas kernels, plane_all_gather(): pl.pallas_call(ag_kernel, out_shape=jax.ShapeDtypeStruct((nx, nz, rows, w...  44.3 us
    all_to_all x1, starting transfers between devices, per_device(): lax.all_to_all(owned, EXPERT_AXES, split_axis=0, concat_axis=0, tiled=True)  17 us
    all_to_all x1, waiting for transfers between devices, per_device(): lax.all_to_all(owned, EXPERT_AXES, split_axis=0, concat_axis=0, tiled=True)  12 us
    dot_general x1, matrix products, per_device(): jnp.dot(expert_rows, w_gate[0], preferred_element_type=jnp.float32)  7.6 us
    all_to_all x1, waiting for transfers between devices, per_device(): lax.all_to_all(slab, EXPERT_AXES, split_axis=0, concat_axis=0, tiled=True)  7.1 us
    dot_general x1, matrix products, per_device(): up_proj = jnp.dot(expert_rows, w_up[0], preferred_element_type=jnp.float32)  6.42 us
    dot_general x1, matrix products, per_device(): jnp.dot(hidden, w_down[0], preferred_element_type=jnp.float32)  6.36 us
  transfers between devices with their start and end apart: 2, of which 2 were waited for; matrix products, arithmetic and copies ran while one was open for 1% of the time, Pallas kernels for 0%

profile of v3, /device:TPU:1, one launch (start us, length us, event | category | flops | bytes accessed | tf_op | source)
XLA Modules:
  0.0 188.5 jit_solution(17956366355363220833)
XLA Ops:
  0.0 0.8 copy.10
  0.8 0.1 reshape.80
  0.8 0.1 fusion.13
  0.9 0.2 select_reduce_fusion
  1.1 1.0 broadcast_in_dim.17
  2.1 0.1 reshape.81
  2.2 0.2 convolution_convert_fusion
  2.5 0.9 reshape.82
  3.4 6.0 %all-to-all-start = ((bf16[8,4,6144]{2,1,0:T(4,128)(2,1)}), bf16[8,4,6144]{2,1,0:T(4,128)(2,1)S(1)}, u32[]{:S(2)}, u32[]{:S(2)}) async-start(bf16[8,4,6144]{2,1,0:T(4,128)(2,1)} %reshape.82), calls=%async_computation | async-start | bytes 786432 | tf_op jit(solution)/shard_map/all_to_all | solution.py:285
  9.3 0.1 reduce_sum.23
  9.4 0.1 mul.46
  9.5 0.7 rev.3
  10.2 7.1 %all-to-all-done = bf16[8,4,6144]{2,1,0:T(4,128)(2,1)S(1)} async-done(((bf16[8,4,6144]{2,1,0:T(4,128)(2,1)}), bf16[8,4,6144]{2,1,0:T(4,128)(2,1)S(1)}, u32[]{:S(2)}, u32[]{:S(2)}) %all-to-all-start) | async-done | bytes 393248 | tf_op jit(solution)/shard_map/all_to_all | solution.py:285
  17.3 0.9 reshape.83.in_ref
  18.2 44.3 %shard_map.64 = bf16[4,4,32,6144]{3,2,1,0:T(8,128)(2,1)} custom-call(bf16[32,6144]{1,0:T(8,128)(2,1)} %reshape.83.in_ref), custom_call_target="tpu_custom_call" | custom-call | tf_op jit(solution)/shard_map/pallas_call | solution.py:239
  62.4 0.0 copy-start
  62.5 0.0 slice-start
  62.5 7.6 %fusion.4 = f32[512,512]{1,0:T(8,128)S(1)} fusion(bf16[512,6144]{1,0:T(8,128)(2,1)} %bitcast.29, bf16[1,6144,512]{2,1,0:T(8,128)(2,1)} %param.9), kind=kOutput, calls=%fused_computation.6 | convolution fusion | flops 3221225472 | bytes 13631488 | tf_op jit(solution)/shard_map/dot_general | solution.py:292
  70.1 0.0 copy-done
  70.1 0.0 slice-start.1
  70.1 6.4 %fusion.9 = bf16[512,512]{1,0:T(8,128)(2,1)S(1)} fusion(bf16[512,6144]{1,0:T(8,128)(2,1)S(1)} %bitcast.30, bf16[1,6144,512]{2,1,0:T(8,128)(2,1)} %param.10, f32[512,512]{1,0:T(8,128)S(1)} %fusion.4), kind=kOutput, calls=%fused_computation.9 | convolution fusion | flops 3222798336 | bytes 14155776 | tf_op jit(solution)/shard_map/dot_general | solution.py:293
  76.5 0.0 slice-done
  76.5 0.0 slice-done.1
  76.6 6.4 %fusion.p_ref = f32[4,4,32,6144]{3,2,1,0:T(8,128)} fusion(bf16[4,4,32,512]{3,2,1,0:T(8,128)(2,1)S(1)} %bitcast.33, bf16[1,512,6144]{2,1,0:T(8,128)(2,1)S(1)} %bitcast.32), kind=kOutput, calls=%fused_computation.2 | convolution fusion | flops 3221225472 | bytes 19398656 | tf_op jit(solution)/shard_map/dot_general | solution.py:295
  82.9 0.0 copy-start.1
  82.9 71.7 %shard_map.65 = f32[32,6144]{1,0:T(8,128)} custom-call(f32[4,4,32,6144]{3,2,1,0:T(8,128)} %fusion.p_ref), custom_call_target="tpu_custom_call" | custom-call | tf_op jit(solution)/shard_map/pallas_call | solution.py:132
  154.6 2.2 %reshape.85 = f32[8,4,6144]{2,1,0:T(4,128)} reshape(f32[32,6144]{1,0:T(8,128)} %shard_map.65) | data formatting | bytes 1572864 | tf_op jit(solution)/shard_map/reshape | solution.py:300
  156.8 17.0 %all-to-all-start.1 = ((f32[8,4,6144]{2,1,0:T(4,128)}), f32[8,4,6144]{2,1,0:T(4,128)S(1)}, u32[]{:S(2)}, u32[]{:S(2)}) async-start(f32[8,4,6144]{2,1,0:T(4,128)} %reshape.85), calls=%async_computation.1 | async-start | bytes 1572864 | tf_op jit(solution)/shard_map/all_to_all | solution.py:301
  173.9 0.0 copy-done.1
  173.9 0.1 copy.12
  174.0 12.0 %all-to-all-done.1 = f32[8,4,6144]{2,1,0:T(4,128)S(1)} async-done(((f32[8,4,6144]{2,1,0:T(4,128)}), f32[8,4,6144]{2,1,0:T(4,128)S(1)}, u32[]{:S(2)}, u32[]{:S(2)}) %all-to-all-start.1) | async-done | bytes 786464 | tf_op jit(solution)/shard_map/all_to_all | solution.py:301
  186.0 0.3 reshape.86
  186.3 0.7 gather_fusion
  187.0 0.2 gather.7
  187.2 1.2 multiply_reduce_fusion
  (8 shorter events, 0.1 us)
Async XLA Ops:
  3.4 13.9 %all-to-all-start = ((bf16[8,4,6144]{2,1,0:T(4,128)(2,1)}), bf16[8,4,6144]{2,1,0:T(4,128)(2,1)S(1)}, u32[]{:S(2)}, u32[]{:S(2)}) async-start(bf16[8,4,6144]{2,1,0:T(4,128)(2,1)} %reshape.82), calls=%async_computation | async-start | bytes 786432 | tf_op jit(solution)/shard_map/all_to_all | solution.py:285
  62.4 7.6 %copy-start = (bf16[4,4,32,6144]{3,2,1,0:T(8,128)(2,1)S(1)}, bf16[4,4,32,6144]{3,2,1,0:T(8,128)(2,1)}, u32[]{:S(2)}) copy-start(bf16[4,4,32,6144]{3,2,1,0:T(8,128)(2,1)} %shard_map.64) | copy-start | bytes 18874372
  62.5 14.1 %slice-start = ((s8[6291456]{0:T(1024)(128)(4,1)}), s8[4194304]{0:T(1024)(128)(4,1)S(1)}, s32[]{:S(2)}) async-start(s8[6291456]{0:T(1024)(128)(4,1)} %bitcast.31), calls=%async_computation.2 | async-start | bytes 8388608
  70.1 6.5 %slice-start.1 = ((s8[6291456]{0:T(1024)(128)(4,1)}), s8[2097152]{0:T(1024)(128)(4,1)S(1)}, s32[]{:S(2)}) async-start(s8[6291456]{0:T(1024)(128)(4,1)} %bitcast.31), calls=%async_computation.3 | async-start | bytes 4194304
  82.9 90.9 %copy-start.1 = (f32[8,2]{0,1:T(2,128)S(1)}, f32[8,2]{0,1:T(2,128)}, u32[]{:S(2)}) copy-start(f32[8,2]{0,1:T(2,128)} %param.7) | copy-start | bytes 196
  156.8 29.2 %all-to-all-start.1 = ((f32[8,4,6144]{2,1,0:T(4,128)}), f32[8,4,6144]{2,1,0:T(4,128)S(1)}, u32[]{:S(2)}, u32[]{:S(2)}) async-start(f32[8,4,6144]{2,1,0:T(4,128)} %reshape.85), calls=%async_computation.1 | async-start | bytes 1572864 | tf_op jit(solution)/shard_map/all_to_all | solution.py:301

commit v4 on v3

--- a/solution.py
+++ b/solution.py
@@ -1,3 +1,5 @@
+import functools
+
 import jax
 import jax.numpy as jnp
 import numpy as np
@@ -10,8 +12,10 @@
 MESH_ID = pl.DeviceIdType.MESH
 
 
-def rs_kernel(p_ref, out_ref, s1, s2, send1, recv1, send2, recv2):
+def rs_kernel(nsect, ny, p_ref, out_ref, fin, s1, s2, send1, recv1, send2, recv2, local_sem, ret_send, ret_recv):
     nx, nz, rows, width = p_ref.shape
+    groups = nsect * ny
+    slots = rows // groups
     quarter = width // 4
     c = lax.axis_index("sect")
     y = lax.axis_index("ey")
@@ -23,11 +27,19 @@
             return (c, y, mx, lax.rem(mz + d + nz, nz))
         return (c, y, lax.rem(mx + d + nx, nx), mz)
 
+    me_group = c * ny + y
+
+    def peer(o):
+        g = lax.rem(me_group + o, groups)
+        return (g // ny, lax.rem(g, ny), mx, mz)
+
     barrier = pltpu.get_barrier_semaphore()
     for axis in ("x", "z"):
         for d in (1, -1):
             pl.semaphore_signal(barrier, inc=1, device_id=dev(axis, d), device_id_type=MESH_ID)
-    pl.semaphore_wait(barrier, 4)
+    for o in range(1, groups):
+        pl.semaphore_signal(barrier, inc=1, device_id=peer(o), device_id_type=MESH_ID)
+    pl.semaphore_wait(barrier, 4 + groups - 1)
 
     rings = [("z", 1), ("z", -1), ("x", 1), ("x", -1)]
 
@@ -82,18 +94,18 @@
         for t in range(lead):
             slot_ref[t] += own_ref[t]
 
-    copies1, n1 = run_phase(lambda r: rings[r][0], own1, s1, send1, recv1, 4)
+    copies1, n1 = run_phase(lambda r: rings[r][0], own1, s1, send1, recv1, nx)
     for r in range(4):
         copies1[(r, n1 - 2)].wait_recv()
         axis = rings[r][0]
-        add_own(s1.at[r, n1 - 2], own1(r, me_on(axis)), 4)
+        add_own(s1.at[r, n1 - 2], own1(r, me_on(axis)), nx)
 
     def own2b(r, i):
         return s1.at[r, n1 - 2, i]
 
     def run_phase2():
         copies = {}
-        n = 4
+        n = nx
         for s in range(n - 1):
             for r in range(4):
                 axis, d = other(rings[r][0]), rings[r][1]
@@ -121,26 +133,50 @@
     for r in range(4):
         copies2[(r, n2 - 2)].wait_recv()
         axis = other(rings[r][0])
-        out_ref[:, cols(r)] = s2[r, n2 - 2] + own2b(r, me_on(axis))[...]
-    for cp in list(copies1.values()) + list(copies2.values()):
+        fin[:, cols(r)] = s2[r, n2 - 2] + own2b(r, me_on(axis))[...]
+    mine = pl.ds(pl.multiple_of(me_group * slots, slots), slots)
+    local = pltpu.make_async_copy(fin.at[mine], out_ref.at[mine], local_sem)
+    local.start()
+    returns = []
+    for o in range(1, groups):
+        g = lax.rem(me_group + o, groups)
+        cp = pltpu.make_async_remote_copy(
+            src_ref=fin.at[pl.ds(pl.multiple_of(g * slots, slots), slots)],
+            dst_ref=out_ref.at[mine],
+            send_sem=ret_send.at[o],
+            recv_sem=ret_recv.at[o],
+            device_id=peer(o),
+            device_id_type=MESH_ID,
+        )
+        cp.start()
+        returns.append(cp)
+    local.wait()
+    for cp in returns:
+        cp.wait_recv()
+    for cp in list(copies1.values()) + list(copies2.values()) + returns:
         cp.wait_send()
 
 
-def plane_reduce_scatter(partial):
+def plane_reduce_scatter(partial, nsect, ny):
     nx, nz, rows, width = partial.shape
     quarter = width // 4
+    groups = nsect * ny
     return pl.pallas_call(
-        rs_kernel,
+        functools.partial(rs_kernel, nsect, ny),
         out_shape=jax.ShapeDtypeStruct((rows, width), jnp.float32),
         in_specs=[pl.BlockSpec(memory_space=pltpu.VMEM)],
         out_specs=pl.BlockSpec(memory_space=pltpu.VMEM),
         scratch_shapes=[
+            pltpu.VMEM((rows, width), jnp.float32),
             pltpu.VMEM((4, nz - 1, nx, rows, quarter), jnp.float32),
             pltpu.VMEM((4, nx - 1, rows, quarter), jnp.float32),
             pltpu.SemaphoreType.DMA((4, nz - 1)),
             pltpu.SemaphoreType.DMA((4, nz - 1)),
             pltpu.SemaphoreType.DMA((4, nx - 1)),
             pltpu.SemaphoreType.DMA((4, nx - 1)),
+            pltpu.SemaphoreType.DMA(()),
+            pltpu.SemaphoreType.DMA((groups,)),
+            pltpu.SemaphoreType.DMA((groups,)),
         ],
         compiler_params=pltpu.CompilerParams(
             collective_id=0, has_side_effects=True, vmem_limit_bytes=60 * 1024 * 1024
@@ -296,10 +332,7 @@
     partial_value = partial_value.reshape(
         nx, plane_count // nx, experts_all * capacity, model_width
     )
-    owned = plane_reduce_scatter(partial_value)
-    owned = owned.reshape(experts_all, capacity, model_width)
-    returned = lax.all_to_all(owned, EXPERT_AXES, split_axis=0, concat_axis=0, tiled=True)
-    expert_out = returned.reshape(experts_all * capacity, model_width)
+    expert_out = plane_reduce_scatter(partial_value, lax.axis_size("sect"), lax.axis_size("ey"))
     weights = jax.nn.sigmoid(router_logits - router_logits[:, ::-1]).reshape(-1)
     picked = jnp.take(expert_out, columns, axis=0) * weights[:, None]
     mixture = jnp.sum(picked.reshape(token_count, 2, model_width), axis=1)

time: 189 us -> 187 us (0.989)
  Pallas kernels: 116 us -> 143 us
  starting transfers between devices: 23 us -> 5.97 us
  waiting for transfers between devices: 19.1 us -> 6.3 us
    pallas_call x1, Pallas kernels: 71.7 us -> 98.3 us  [plane_reduce_scatter(): pl.pallas_call(functools.partial(rs_kernel, nsect, ny), out_shape=jax.Sha...]
    all_to_all x1 -> x0, starting transfers between devices: 17 us -> none  [per_device(): lax.all_to_all(owned, EXPERT_AXES, split_axis=0, concat_axis=0, tiled=True)]
    all_to_all x1 -> x0, waiting for transfers between devices: 12 us -> none  [per_device(): lax.all_to_all(owned, EXPERT_AXES, split_axis=0, concat_axis=0, tiled=True)]
    reshape x2 -> x0, local copies, waits for them, and re-layouts: 2.51 us -> none  [the longest x1 2.24 us: per_device(): owned = owned.reshape(experts_all, capacity, model_width)]
  transfers between devices with their start and end apart: 2 -> 1, of which waited for: 2 -> 1; matrix products, arithmetic and copies ran while one was open for 1% -> 1% of each run, Pallas kernels for 0% -> 0%
where the time goes in v4:
time: 187 us; the launch traced here: 185 us
  Pallas kernels  143 us (76%)
  matrix products  20.7 us (11%)
  local copies, waits for them, and re-layouts  6.83 us (4%)
  waiting for transfers between devices  6.3 us (3%)
  starting transfers between devices  5.97 us (3%)
  other arithmetic  2.26 us (1%)
    pallas_call x1, Pallas kernels, plane_reduce_scatter(): pl.pallas_call(functools.partial(rs_kernel, nsect, ny), out_shape=jax.Sha...  98.3 us
    pallas_call x1, Pallas kernels, plane_all_gather(): pl.pallas_call(ag_kernel, out_shape=jax.ShapeDtypeStruct((nx, nz, rows, w...  44.3 us
    dot_general x1, matrix products, per_device(): jnp.dot(expert_rows, w_gate[0], preferred_element_type=jnp.float32)  7.6 us
    dot_general x1, matrix products, per_device(): up_proj = jnp.dot(expert_rows, w_up[0], preferred_element_type=jnp.float32)  6.47 us
    dot_general x1, matrix products, per_device(): jnp.dot(hidden, w_down[0], preferred_element_type=jnp.float32)  6.42 us
    all_to_all x1, waiting for transfers between devices, per_device(): lax.all_to_all(slab, EXPERT_AXES, split_axis=0, concat_axis=0, tiled=True)  6.3 us
    all_to_all x1, starting transfers between devices, per_device(): lax.all_to_all(slab, EXPERT_AXES, split_axis=0, concat_axis=0, tiled=True)  5.97 us
  transfers between devices with their start and end apart: 1, of which 1 were waited for; matrix products, arithmetic and copies ran while one was open for 1% of the time, Pallas kernels for 0%

profile of v4, /device:TPU:1, one launch (start us, length us, event | category | flops | bytes accessed | tf_op | source)
XLA Modules:
  0.0 184.8 jit_solution(3639178371325573629)
XLA Ops:
  0.0 0.8 copy.10
  0.8 0.1 reshape.74
  0.8 0.1 fusion.13
  0.9 0.2 select_reduce_fusion
  1.1 1.0 broadcast_in_dim.17
  2.1 0.1 reshape.75
  2.2 0.2 convolution_convert_fusion
  2.5 0.9 reshape.76
  3.4 6.0 %all-to-all-start = ((bf16[8,4,6144]{2,1,0:T(4,128)(2,1)}), bf16[8,4,6144]{2,1,0:T(4,128)(2,1)S(1)}, u32[]{:S(2)}, u32[]{:S(2)}) async-start(bf16[8,4,6144]{2,1,0:T(4,128)(2,1)} %reshape.76), calls=%async_computation | async-start | bytes 786432 | tf_op jit(solution)/shard_map/all_to_all | solution.py:321
  9.3 0.1 mul.46
  9.4 0.7 rev.3
  10.1 0.7 add_divide_fusion
  10.8 0.1 reduce_sum.23
  10.9 0.1 copy.12
  11.0 6.3 %all-to-all-done = bf16[8,4,6144]{2,1,0:T(4,128)(2,1)S(1)} async-done(((bf16[8,4,6144]{2,1,0:T(4,128)(2,1)}), bf16[8,4,6144]{2,1,0:T(4,128)(2,1)S(1)}, u32[]{:S(2)}, u32[]{:S(2)}) %all-to-all-start) | async-done | bytes 393248 | tf_op jit(solution)/shard_map/all_to_all | solution.py:321
  17.3 0.9 reshape.77.in_ref
  18.2 44.3 %shard_map.64 = bf16[4,4,32,6144]{3,2,1,0:T(8,128)(2,1)} custom-call(bf16[32,6144]{1,0:T(8,128)(2,1)} %reshape.77.in_ref), custom_call_target="tpu_custom_call" | custom-call | tf_op jit(solution)/shard_map/pallas_call | solution.py:275
  62.5 0.0 copy-start
  62.5 0.0 slice-start
  62.5 7.6 %fusion.4 = f32[512,512]{1,0:T(8,128)S(1)} fusion(bf16[512,6144]{1,0:T(8,128)(2,1)} %bitcast.29, bf16[1,6144,512]{2,1,0:T(8,128)(2,1)} %param.9), kind=kOutput, calls=%fused_computation.6 | convolution fusion | flops 3221225472 | bytes 13631488 | tf_op jit(solution)/shard_map/dot_general | solution.py:328
  70.1 0.0 copy-done
  70.1 0.0 slice-start.1
  70.1 6.5 %fusion.9 = bf16[512,512]{1,0:T(8,128)(2,1)S(1)} fusion(bf16[512,6144]{1,0:T(8,128)(2,1)S(1)} %bitcast.30, bf16[1,6144,512]{2,1,0:T(8,128)(2,1)} %param.10, f32[512,512]{1,0:T(8,128)S(1)} %fusion.4), kind=kOutput, calls=%fused_computation.9 | convolution fusion | flops 3222798336 | bytes 14155776 | tf_op jit(solution)/shard_map/dot_general | solution.py:329
  76.6 0.0 slice-done
  76.6 0.0 slice-done.1
  76.6 6.4 %fusion.p_ref = f32[4,4,32,6144]{3,2,1,0:T(8,128)} fusion(bf16[4,4,32,512]{3,2,1,0:T(8,128)(2,1)S(1)} %bitcast.33, bf16[1,512,6144]{2,1,0:T(8,128)(2,1)S(1)} %bitcast.32), kind=kOutput, calls=%fused_computation.2 | convolution fusion | flops 3221225472 | bytes 19398656 | tf_op jit(solution)/shard_map/dot_general | solution.py:331
  83.1 98.3 %shard_map.65 = f32[32,6144]{1,0:T(8,128)} custom-call(f32[4,4,32,6144]{3,2,1,0:T(8,128)} %fusion.p_ref), custom_call_target="tpu_custom_call" | custom-call | tf_op jit(solution)/shard_map/pallas_call | solution.py:164
  181.3 2.0 %gather_fusion = f32[16,6144]{1,0:T(8,128)S(1)} fusion(f32[32,6144]{1,0:T(8,128)} %shard_map.65, s32[1024]{0:T(1024)S(1)} %pad_clamp_fusion), kind=kCustom, calls=%fused_computation | custom fusion | bytes 786496 | tf_op jit(solution)/shard_map/jit(_take)/gather | solution.py:337
  183.3 0.2 gather.7
  183.6 1.2 multiply_reduce_fusion
  (7 shorter events, 0.1 us)
Async XLA Ops:
  3.4 13.9 %all-to-all-start = ((bf16[8,4,6144]{2,1,0:T(4,128)(2,1)}), bf16[8,4,6144]{2,1,0:T(4,128)(2,1)S(1)}, u32[]{:S(2)}, u32[]{:S(2)}) async-start(bf16[8,4,6144]{2,1,0:T(4,128)(2,1)} %reshape.76), calls=%async_computation | async-start | bytes 786432 | tf_op jit(solution)/shard_map/all_to_all | solution.py:321
  62.5 7.6 %copy-start = (bf16[4,4,32,6144]{3,2,1,0:T(8,128)(2,1)S(1)}, bf16[4,4,32,6144]{3,2,1,0:T(8,128)(2,1)}, u32[]{:S(2)}) copy-start(bf16[4,4,32,6144]{3,2,1,0:T(8,128)(2,1)} %shard_map.64) | copy-start | bytes 18874372
  62.5 14.1 %slice-start = ((s8[6291456]{0:T(1024)(128)(4,1)}), s8[4194304]{0:T(1024)(128)(4,1)S(1)}, s32[]{:S(2)}) async-start(s8[6291456]{0:T(1024)(128)(4,1)} %bitcast.31), calls=%async_computation.1 | async-start | bytes 8388608
  70.1 6.5 %slice-start.1 = ((s8[6291456]{0:T(1024)(128)(4,1)}), s8[2097152]{0:T(1024)(128)(4,1)S(1)}, s32[]{:S(2)}) async-start(s8[6291456]{0:T(1024)(128)(4,1)} %bitcast.31), calls=%async_computation.2 | async-start | bytes 4194304

commit v5 on v4

--- a/solution.py
+++ b/solution.py
@@ -12,15 +12,26 @@
 MESH_ID = pl.DeviceIdType.MESH
 
 
-def rs_kernel(nsect, ny, p_ref, out_ref, fin, s1, s2, send1, recv1, send2, recv2, local_sem, ret_send, ret_recv):
-    nx, nz, rows, width = p_ref.shape
+def rs_kernel(
+    nsect, ny, rows_ref, wg_hbm, wu_hbm, wd_hbm, out_ref,
+    wg, wu, wd, hid, stage, fin, s1, s2, wsem, send1, recv1, send2, recv2, local_sem, ret_send, ret_recv,
+):
+    nx, nz, rows, width = rows_ref.shape
+    hidden_width = wd.shape[0]
+    quarter = width // 4
     groups = nsect * ny
     slots = rows // groups
-    quarter = width // 4
     c = lax.axis_index("sect")
     y = lax.axis_index("ey")
     mx = lax.axis_index("ex")
     mz = lax.axis_index("tp")
+
+    weight_copies = [
+        pltpu.make_async_copy(src, dst, wsem.at[i])
+        for i, (src, dst) in enumerate(((wg_hbm, wg), (wu_hbm, wu), (wd_hbm, wd)))
+    ]
+    for cp in weight_copies:
+        cp.start()
 
     def dev(axis, d):
         if axis == "z":
@@ -41,99 +52,98 @@
         pl.semaphore_signal(barrier, inc=1, device_id=peer(o), device_id_type=MESH_ID)
     pl.semaphore_wait(barrier, 4 + groups - 1)
 
+    weight_copies[0].wait()
+    weight_copies[1].wait()
+
+    def hidden_group(i, carry):
+        block = rows_ref[i].reshape(nz * rows, width)
+        gate = jnp.dot(block, wg[...], preferred_element_type=jnp.float32)
+        up = jnp.dot(block, wu[...], preferred_element_type=jnp.float32)
+        act = (jax.nn.silu(gate) * up).astype(hid.dtype)
+        hid[i] = act.reshape(nz, rows, hidden_width)
+        return carry
+
+    lax.fori_loop(0, nx, hidden_group, 0)
+    weight_copies[2].wait()
+
     rings = [("z", 1), ("z", -1), ("x", 1), ("x", -1)]
 
     def me_on(axis):
         return mz if axis == "z" else mx
 
-    def size_on(axis):
-        return nz if axis == "z" else nx
-
     def cols(r):
         return pl.ds(r * quarter, quarter)
 
-    def own1(r, j):
+    def chunk(r, j):
         if rings[r][0] == "z":
-            return p_ref.at[:, j, :, cols(r)]
-        return p_ref.at[j, :, :, cols(r)]
-
-    def own2(r, i):
-        return s1.at[r, size_on(rings[r][0]) - 2, i]
+            h = hid[:, j]
+        else:
+            h = hid[j]
+        lead = h.shape[0]
+        part = jnp.dot(
+            h.reshape(lead * rows, hidden_width), wd[:, cols(r)], preferred_element_type=jnp.float32
+        )
+        return part.reshape(lead, rows, quarter)
 
     def other(axis):
         return "x" if axis == "z" else "z"
 
-    def run_phase(axis_of, own, slots, send, recv, lead):
-        copies = {}
-        n = size_on(axis_of(0))
-        for s in range(n - 1):
-            for r in range(4):
-                axis, d = axis_of(r), rings[r][1]
-                me = me_on(axis)
-                j = lax.rem(me + n * (s + 2) - d * (s + 1), n)
-                if s == 0:
-                    src = own(r, j)
-                else:
-                    copies[(r, s - 1)].wait_recv()
-                    for t in range(lead):
-                        slots[r, s - 1, t] += own(r, j)[t]
-                    src = slots.at[r, s - 1]
-                cp = pltpu.make_async_remote_copy(
-                    src_ref=src,
-                    dst_ref=slots.at[r, s],
-                    send_sem=send.at[r, s],
-                    recv_sem=recv.at[r, s],
-                    device_id=dev(axis, d),
-                    device_id_type=MESH_ID,
-                )
-                cp.start()
-                copies[(r, s)] = cp
-        return copies, n
-
-    def add_own(slot_ref, own_ref, lead):
-        for t in range(lead):
-            slot_ref[t] += own_ref[t]
-
-    copies1, n1 = run_phase(lambda r: rings[r][0], own1, s1, send1, recv1, nx)
+    n1 = nz
+    copies1 = {}
+    for s in range(n1 - 1):
+        for r in range(4):
+            axis, d = rings[r][0], rings[r][1]
+            j = lax.rem(me_on(axis) + n1 * (s + 2) - d * (s + 1), n1)
+            if s == 0:
+                stage[r] = chunk(r, j)
+                src = stage.at[r]
+            else:
+                part = chunk(r, j)
+                copies1[(r, s - 1)].wait_recv()
+                s1[r, s - 1] = s1[r, s - 1] + part
+                src = s1.at[r, s - 1]
+            cp = pltpu.make_async_remote_copy(
+                src_ref=src,
+                dst_ref=s1.at[r, s],
+                send_sem=send1.at[r, s],
+                recv_sem=recv1.at[r, s],
+                device_id=dev(axis, d),
+                device_id_type=MESH_ID,
+            )
+            cp.start()
+            copies1[(r, s)] = cp
     for r in range(4):
+        part = chunk(r, me_on(rings[r][0]))
         copies1[(r, n1 - 2)].wait_recv()
-        axis = rings[r][0]
-        add_own(s1.at[r, n1 - 2], own1(r, me_on(axis)), nx)
-
-    def own2b(r, i):
-        return s1.at[r, n1 - 2, i]
-
-    def run_phase2():
-        copies = {}
-        n = nx
-        for s in range(n - 1):
-            for r in range(4):
-                axis, d = other(rings[r][0]), rings[r][1]
-                me = me_on(axis)
-                j = lax.rem(me + n * (s + 2) - d * (s + 1), n)
-                if s == 0:
-                    src = own2b(r, j)
-                else:
-                    copies[(r, s - 1)].wait_recv()
-                    s2[r, s - 1] += own2b(r, j)[...]
-                    src = s2.at[r, s - 1]
-                cp = pltpu.make_async_remote_copy(
-                    src_ref=src,
-                    dst_ref=s2.at[r, s],
-                    send_sem=send2.at[r, s],
-                    recv_sem=recv2.at[r, s],
-                    device_id=dev(axis, d),
-                    device_id_type=MESH_ID,
-                )
-                cp.start()
-                copies[(r, s)] = cp
-        return copies, n
-
-    copies2, n2 = run_phase2()
+        s1[r, n1 - 2] = s1[r, n1 - 2] + part
+
+    n2 = nx
+    copies2 = {}
+    for s in range(n2 - 1):
+        for r in range(4):
+            axis, d = other(rings[r][0]), rings[r][1]
+            j = lax.rem(me_on(axis) + n2 * (s + 2) - d * (s + 1), n2)
+            if s == 0:
+                src = s1.at[r, n1 - 2, j]
+            else:
+                copies2[(r, s - 1)].wait_recv()
+                s2[r, s - 1] += s1[r, n1 - 2, j]
+                src = s2.at[r, s - 1]
+            cp = pltpu.make_async_remote_copy(
+                src_ref=src,
+                dst_ref=s2.at[r, s],
+                send_sem=send2.at[r, s],
+                recv_sem=recv2.at[r, s],
+                device_id=dev(axis, d),
+                device_id_type=MESH_ID,
+            )
+            cp.start()
+            copies2[(r, s)] = cp
     for r in range(4):
         copies2[(r, n2 - 2)].wait_recv()
         axis = other(rings[r][0])
-        fin[:, cols(r)] = s2[r, n2 - 2] + own2b(r, me_on(axis))[...]
+        fin[:, cols(r)] = s2[r, n2 - 2] + s1[r, n1 - 2, me_on(axis)]
+
     mine = pl.ds(pl.multiple_of(me_group * slots, slots), slots)
     local = pltpu.make_async_copy(fin.at[mine], out_ref.at[mine], local_sem)
     local.start()
@@ -157,19 +167,31 @@
         cp.wait_send()
 
 
-def plane_reduce_scatter(partial, nsect, ny):
-    nx, nz, rows, width = partial.shape
+def expert_reduce_scatter(expert_rows, w_gate, w_up, w_down, nsect, ny):
+    nx, nz, rows, width = expert_rows.shape
+    hidden_width = w_down.shape[0]
     quarter = width // 4
     groups = nsect * ny
     return pl.pallas_call(
         functools.partial(rs_kernel, nsect, ny),
         out_shape=jax.ShapeDtypeStruct((rows, width), jnp.float32),
-        in_specs=[pl.BlockSpec(memory_space=pltpu.VMEM)],
+        in_specs=[
+            pl.BlockSpec(memory_space=pltpu.VMEM),
+            pl.BlockSpec(memory_space=pl.ANY),
+            pl.BlockSpec(memory_space=pl.ANY),
+            pl.BlockSpec(memory_space=pl.ANY),
+        ],
         out_specs=pl.BlockSpec(memory_space=pltpu.VMEM),
         scratch_shapes=[
+            pltpu.VMEM(w_gate.shape, w_gate.dtype),
+            pltpu.VMEM(w_up.shape, w_up.dtype),
+            pltpu.VMEM(w_down.shape, w_down.dtype),
+            pltpu.VMEM((nx, nz, rows, hidden_width), jnp.bfloat16),
+            pltpu.VMEM((4, nx, rows, quarter), jnp.float32),
             pltpu.VMEM((rows, width), jnp.float32),
             pltpu.VMEM((4, nz - 1, nx, rows, quarter), jnp.float32),
             pltpu.VMEM((4, nx - 1, rows, quarter), jnp.float32),
+            pltpu.SemaphoreType.DMA((3,)),
             pltpu.SemaphoreType.DMA((4, nz - 1)),
             pltpu.SemaphoreType.DMA((4, nz - 1)),
             pltpu.SemaphoreType.DMA((4, nx - 1)),
@@ -179,9 +201,10 @@
             pltpu.SemaphoreType.DMA((groups,)),
         ],
         compiler_params=pltpu.CompilerParams(
-            collective_id=0, has_side_effects=True, vmem_limit_bytes=60 * 1024 * 1024
+            collective_id=0, has_side_effects=True, vmem_limit_bytes=64 * 1024 * 1024
         ),
-    )(partial)
+    )(expert_rows, w_gate, w_up, w_down)
+
 
 def ag_kernel(in_ref, out_ref, local_sem, send1, recv1, send2, recv2):
     nx, nz, rows, width = out_ref.shape
@@ -323,16 +346,9 @@
     plane_rows = plane_all_gather(
         column_rows.reshape(experts_all * capacity, model_width), nx, plane_count // nx
     )
-    row_count = plane_count * experts_all * capacity
-    expert_rows = plane_rows.reshape(row_count, model_width)
-    gate_proj = jnp.dot(expert_rows, w_gate[0], preferred_element_type=jnp.float32)
-    up_proj = jnp.dot(expert_rows, w_up[0], preferred_element_type=jnp.float32)
-    hidden = (jax.nn.silu(gate_proj) * up_proj).astype(jnp.bfloat16)
-    partial_value = jnp.dot(hidden, w_down[0], preferred_element_type=jnp.float32)
-    partial_value = partial_value.reshape(
-        nx, plane_count // nx, experts_all * capacity, model_width
-    )
-    expert_out = plane_reduce_scatter(partial_value, lax.axis_size("sect"), lax.axis_size("ey"))
+    expert_out = expert_reduce_scatter(
+        plane_rows, w_gate[0], w_up[0], w_down[0], lax.axis_size("sect"), lax.axis_size("ey")
+    )
     weights = jax.nn.sigmoid(router_logits - router_logits[:, ::-1]).reshape(-1)
     picked = jnp.take(expert_out, columns, axis=0) * weights[:, None]
     mixture = jnp.sum(picked.reshape(token_count, 2, model_width), axis=1)

time: 187 us -> 173 us (0.925)
  matrix products: 20.7 us -> 0.24 us
  Pallas kernels: 143 us -> 149 us
    dot_general x3 -> x0, matrix products: 20.5 us -> none  [the longest x1 7.6 us: per_device(): jnp.dot(expert_rows, w_gate[0], preferred_element_type=jnp.float32)]
    pallas_call x1, Pallas kernels: 98.3 us -> 105 us  [expert_reduce_scatter(): pl.pallas_call(functools.partial(rs_kernel, nsect, ny), out_shape=jax.Sha...]
  transfers between devices with their start and end apart: 1 -> 1, of which waited for: 1 -> 1; matrix products, arithmetic and copies ran while one was open for 1% -> 2% of each run, Pallas kernels for 0% -> 0%
where the time goes in v5:
time: 173 us; the launch traced here: 172 us
  Pallas kernels  149 us (86%)
  local copies, waits for them, and re-layouts  7.54 us (4%)
  starting transfers between devices  5.97 us (3%)
  waiting for transfers between devices  4.57 us (3%)
  other arithmetic  4.09 us (2%)
    pallas_call x1, Pallas kernels, expert_reduce_scatter(): pl.pallas_call(functools.partial(rs_kernel, nsect, ny), out_shape=jax.Sha...  105 us
    pallas_call x1, Pallas kernels, plane_all_gather(): pl.pallas_call(ag_kernel, out_shape=jax.ShapeDtypeStruct((nx, nz, rows, w...  44.3 us
    all_to_all x1, starting transfers between devices, per_device(): lax.all_to_all(slab, EXPERT_AXES, split_axis=0, concat_axis=0, tiled=True)  5.97 us
    all_to_all x1, waiting for transfers between devices, per_device(): lax.all_to_all(slab, EXPERT_AXES, split_axis=0, concat_axis=0, tiled=True)  4.57 us
  transfers between devices with their start and end apart: 1, of which 1 were waited for; matrix products, arithmetic and copies ran while one was open for 2% of the time, Pallas kernels for 0%

profile of v5, /device:TPU:1, one launch (start us, length us, event | category | flops | bytes accessed | tf_op | source)
XLA Modules:
  0.0 171.6 jit_solution(4658555736210995673)
XLA Ops:
  0.0 0.8 copy.10
  0.8 0.1 reshape.69
  0.8 0.1 fusion.1
  0.9 0.2 select_reduce_fusion
  1.1 1.0 broadcast_in_dim.17
  2.1 0.1 reshape.70
  2.2 0.2 convolution_convert_fusion
  2.5 0.9 reshape.71
  3.4 6.0 %all-to-all-start = ((bf16[8,4,6144]{2,1,0:T(4,128)(2,1)}), bf16[8,4,6144]{2,1,0:T(4,128)(2,1)S(1)}, u32[]{:S(2)}, u32[]{:S(2)}) async-start(bf16[8,4,6144]{2,1,0:T(4,128)(2,1)} %reshape.71), calls=%async_computation | async-start | bytes 786432 | tf_op jit(solution)/shard_map/all_to_all | solution.py:344
  9.3 0.1 mul.37
  9.4 0.7 rev.3
  10.1 0.7 add_divide_fusion
  10.8 0.1 reduce_sum.23
  10.9 0.7 copy.12
  11.6 0.6 pad_clamp_fusion
  12.2 0.5 compare_and_fusion
  12.7 4.6 %all-to-all-done = bf16[8,4,6144]{2,1,0:T(4,128)(2,1)S(1)} async-done(((bf16[8,4,6144]{2,1,0:T(4,128)(2,1)}), bf16[8,4,6144]{2,1,0:T(4,128)(2,1)S(1)}, u32[]{:S(2)}, u32[]{:S(2)}) %all-to-all-start) | async-done | bytes 393248 | tf_op jit(solution)/shard_map/all_to_all | solution.py:344
  17.3 0.9 reshape.72.in_ref
  18.2 44.3 %shard_map.64.rows_ref = bf16[4,4,32,6144]{3,2,1,0:T(8,128)(2,1)} custom-call(bf16[32,6144]{1,0:T(8,128)(2,1)} %reshape.72.in_ref), custom_call_target="tpu_custom_call" | custom-call | tf_op jit(solution)/shard_map/pallas_call | solution.py:298
  62.5 104.8 %shard_map.65 = f32[32,6144]{1,0:T(8,128)} custom-call(bf16[4,4,32,6144]{3,2,1,0:T(8,128)(2,1)} %shard_map.64.rows_ref, bf16[6144,512]{1,0:T(8,128)(2,1)} %bitcast.10, bf16[6144,512]{1,0:T(8,128)(2,1)} %bitcast.11, bf16[512,6144]{1,0:T(8,128)(2,1)} %bitcast.12), custom_call_target="tpu_custom_call" | custom-call | tf_op jit(solution)/shard_map/pallas_call | solution.py:175
  167.3 2.1 %gather_fusion = f32[16,6144]{1,0:T(8,128)S(1)} fusion(f32[32,6144]{1,0:T(8,128)} %shard_map.65, s32[1024]{0:T(1024)} %pad_clamp_fusion), kind=kCustom, calls=%fused_computation | custom fusion | bytes 786496 | tf_op jit(solution)/shard_map/jit(_take)/gather | solution.py:353
  169.4 0.2 gather.7
  169.7 1.9 %multiply_reduce_fusion = bf16[8,6144]{1,0:T(8,128)(2,1)} fusion(f32[8,2,6144]{2,1,0:T(2,128)S(1)} %gather.7, pred[8,2]{1,0:T(8,128)(4,1)} %compare_and_fusion, f32[8,2]{1,0:T(8,128)} %copy.12), kind=kLoop, calls=%fused_computation.2 | loop fusion | flops 245760 | bytes 491600 | tf_op jit(solution)/shard_map/reduce_sum | solution.py:354
  (4 shorter events, 0.1 us)
Async XLA Ops:
  3.4 13.9 %all-to-all-start = ((bf16[8,4,6144]{2,1,0:T(4,128)(2,1)}), bf16[8,4,6144]{2,1,0:T(4,128)(2,1)S(1)}, u32[]{:S(2)}, u32[]{:S(2)}) async-start(bf16[8,4,6144]{2,1,0:T(4,128)(2,1)} %reshape.71), calls=%async_computation | async-start | bytes 786432 | tf_op jit(solution)/shard_map/all_to_all | solution.py:344

commit v6 on v5

--- a/solution.py
+++ b/solution.py
@@ -14,7 +14,7 @@
 
 def rs_kernel(
     nsect, ny, rows_ref, wg_hbm, wu_hbm, wd_hbm, out_ref,
-    wg, wu, wd, hid, stage, fin, s1, s2, wsem, send1, recv1, send2, recv2, local_sem, ret_send, ret_recv,
+    wg, wu, wd, hid, stage, fin, s1, total1, s2, wsem, send1, recv1, send2, recv2, local_sem, ret_send, ret_recv,
 ):
     nx, nz, rows, width = rows_ref.shape
     hidden_width = wd.shape[0]
@@ -95,12 +95,12 @@
             axis, d = rings[r][0], rings[r][1]
             j = lax.rem(me_on(axis) + n1 * (s + 2) - d * (s + 1), n1)
             if s == 0:
-                stage[r] = chunk(r, j)
+                stage[r] = chunk(r, j).astype(stage.dtype)
                 src = stage.at[r]
             else:
                 part = chunk(r, j)
                 copies1[(r, s - 1)].wait_recv()
-                s1[r, s - 1] = s1[r, s - 1] + part
+                s1[r, s - 1] = (s1[r, s - 1].astype(jnp.float32) + part).astype(s1.dtype)
                 src = s1.at[r, s - 1]
             cp = pltpu.make_async_remote_copy(
                 src_ref=src,
@@ -115,7 +115,7 @@
     for r in range(4):
         part = chunk(r, me_on(rings[r][0]))
         copies1[(r, n1 - 2)].wait_recv()
-        s1[r, n1 - 2] = s1[r, n1 - 2] + part
+        total1[r] = s1[r, n1 - 2].astype(jnp.float32) + part
 
     n2 = nx
     copies2 = {}
@@ -124,10 +124,10 @@
             axis, d = other(rings[r][0]), rings[r][1]
             j = lax.rem(me_on(axis) + n2 * (s + 2) - d * (s + 1), n2)
             if s == 0:
-                src = s1.at[r, n1 - 2, j]
+                src = total1.at[r, j]
             else:
                 copies2[(r, s - 1)].wait_recv()
-                s2[r, s - 1] += s1[r, n1 - 2, j]
+                s2[r, s - 1] += total1[r, j]
                 src = s2.at[r, s - 1]
             cp = pltpu.make_async_remote_copy(
                 src_ref=src,
@@ -142,7 +142,7 @@
     for r in range(4):
         copies2[(r, n2 - 2)].wait_recv()
         axis = other(rings[r][0])
-        fin[:, cols(r)] = s2[r, n2 - 2] + s1[r, n1 - 2, me_on(axis)]
+        fin[:, cols(r)] = s2[r, n2 - 2] + total1[r, me_on(axis)]
 
     mine = pl.ds(pl.multiple_of(me_group * slots, slots), slots)
     local = pltpu.make_async_copy(fin.at[mine], out_ref.at[mine], local_sem)
@@ -187,9 +187,10 @@
             pltpu.VMEM(w_up.shape, w_up.dtype),
             pltpu.VMEM(w_down.shape, w_down.dtype),
             pltpu.VMEM((nx, nz, rows, hidden_width), jnp.bfloat16),
+            pltpu.VMEM((4, nx, rows, quarter), jnp.bfloat16),
+            pltpu.VMEM((rows, width), jnp.float32),
+            pltpu.VMEM((4, nz - 1, nx, rows, quarter), jnp.bfloat16),
             pltpu.VMEM((4, nx, rows, quarter), jnp.float32),
-            pltpu.VMEM((rows, width), jnp.float32),
-            pltpu.VMEM((4, nz - 1, nx, rows, quarter), jnp.float32),
             pltpu.VMEM((4, nx - 1, rows, quarter), jnp.float32),
             pltpu.SemaphoreType.DMA((3,)),
             pltpu.SemaphoreType.DMA((4, nz - 1)),

time: 173 us -> 150 us (0.87)
  Pallas kernels: 149 us -> 125 us
    pallas_call x1, Pallas kernels: 105 us -> 80.5 us  [expert_reduce_scatter(): pl.pallas_call(functools.partial(rs_kernel, nsect, ny), out_shape=jax.Sha...]
where the time goes in v6:
time: 150 us; the launch traced here: 147 us
  Pallas kernels  125 us (83%)
  local copies, waits for them, and re-layouts  7.54 us (5%)
  starting transfers between devices  5.97 us (4%)
  waiting for transfers between devices  4.57 us (3%)
  other arithmetic  4.09 us (3%)
    pallas_call x1, Pallas kernels, expert_reduce_scatter(): pl.pallas_call(functools.partial(rs_kernel, nsect, ny), out_shape=jax.Sha...  80.5 us
    pallas_call x1, Pallas kernels, plane_all_gather(): pl.pallas_call(ag_kernel, out_shape=jax.ShapeDtypeStruct((nx, nz, rows, w...  44.3 us
    all_to_all x1, starting transfers between devices, per_device(): lax.all_to_all(slab, EXPERT_AXES, split_axis=0, concat_axis=0, tiled=True)  5.97 us
    all_to_all x1, waiting for transfers between devices, per_device(): lax.all_to_all(slab, EXPERT_AXES, split_axis=0, concat_axis=0, tiled=True)  4.57 us
  transfers between devices with their start and end apart: 1, of which 1 were waited for; matrix products, arithmetic and copies ran while one was open for 2% of the time, Pallas kernels for 0%

profile of v6, /device:TPU:1, one launch (start us, length us, event | category | flops | bytes accessed | tf_op | source)
XLA Modules:
  0.0 147.3 jit_solution(6247131468237570995)
XLA Ops:
  0.0 0.8 copy.10
  0.8 0.1 reshape.69
  0.8 0.1 fusion.1
  0.9 0.2 select_reduce_fusion
  1.1 1.0 broadcast_in_dim.17
  2.1 0.1 reshape.70
  2.2 0.2 convolution_convert_fusion
  2.5 0.9 reshape.71
  3.4 6.0 %all-to-all-start = ((bf16[8,4,6144]{2,1,0:T(4,128)(2,1)}), bf16[8,4,6144]{2,1,0:T(4,128)(2,1)S(1)}, u32[]{:S(2)}, u32[]{:S(2)}) async-start(bf16[8,4,6144]{2,1,0:T(4,128)(2,1)} %reshape.71), calls=%async_computation | async-start | bytes 786432 | tf_op jit(solution)/shard_map/all_to_all | solution.py:345
  9.3 0.1 mul.37
  9.4 0.7 rev.3
  10.1 0.7 add_divide_fusion
  10.8 0.1 reduce_sum.23
  10.9 0.7 copy.12
  11.6 0.6 pad_clamp_fusion
  12.2 0.5 compare_and_fusion
  12.7 4.6 %all-to-all-done = bf16[8,4,6144]{2,1,0:T(4,128)(2,1)S(1)} async-done(((bf16[8,4,6144]{2,1,0:T(4,128)(2,1)}), bf16[8,4,6144]{2,1,0:T(4,128)(2,1)S(1)}, u32[]{:S(2)}, u32[]{:S(2)}) %all-to-all-start) | async-done | bytes 393248 | tf_op jit(solution)/shard_map/all_to_all | solution.py:345
  17.3 0.9 reshape.72.in_ref
  18.2 44.3 %shard_map.64.rows_ref = bf16[4,4,32,6144]{3,2,1,0:T(8,128)(2,1)} custom-call(bf16[32,6144]{1,0:T(8,128)(2,1)} %reshape.72.in_ref), custom_call_target="tpu_custom_call" | custom-call | tf_op jit(solution)/shard_map/pallas_call | solution.py:299
  62.5 80.5 %shard_map.65 = f32[32,6144]{1,0:T(8,128)} custom-call(bf16[4,4,32,6144]{3,2,1,0:T(8,128)(2,1)} %shard_map.64.rows_ref, bf16[6144,512]{1,0:T(8,128)(2,1)} %bitcast.10, bf16[6144,512]{1,0:T(8,128)(2,1)} %bitcast.11, bf16[512,6144]{1,0:T(8,128)(2,1)} %bitcast.12), custom_call_target="tpu_custom_call" | custom-call | tf_op jit(solution)/shard_map/pallas_call | solution.py:175
  143.0 2.1 %gather_fusion = f32[16,6144]{1,0:T(8,128)S(1)} fusion(f32[32,6144]{1,0:T(8,128)} %shard_map.65, s32[1024]{0:T(1024)} %pad_clamp_fusion), kind=kCustom, calls=%fused_computation | custom fusion | bytes 786496 | tf_op jit(solution)/shard_map/jit(_take)/gather | solution.py:354
  145.1 0.2 gather.7
  145.3 1.9 %multiply_reduce_fusion = bf16[8,6144]{1,0:T(8,128)(2,1)} fusion(f32[8,2,6144]{2,1,0:T(2,128)S(1)} %gather.7, pred[8,2]{1,0:T(8,128)(4,1)} %compare_and_fusion, f32[8,2]{1,0:T(8,128)} %copy.12), kind=kLoop, calls=%fused_computation.2 | loop fusion | flops 245760 | bytes 491600 | tf_op jit(solution)/shard_map/reduce_sum | solution.py:355
  (4 shorter events, 0.1 us)
Async XLA Ops:
  3.4 13.9 %all-to-all-start = ((bf16[8,4,6144]{2,1,0:T(4,128)(2,1)}), bf16[8,4,6144]{2,1,0:T(4,128)(2,1)S(1)}, u32[]{:S(2)}, u32[]{:S(2)}) async-start(bf16[8,4,6144]{2,1,0:T(4,128)(2,1)} %reshape.71), calls=%async_computation | async-start | bytes 786432 | tf_op jit(solution)/shard_map/all_to_all | solution.py:345

commit v7 on v6

--- a/solution.py
+++ b/solution.py
@@ -207,8 +207,10 @@
     )(expert_rows, w_gate, w_up, w_down)
 
 
-def ag_kernel(in_ref, out_ref, local_sem, send1, recv1, send2, recv2):
+def ag_kernel(nsect, ny, in_ref, out_ref, local_sem, in_send, in_recv, send1, recv1, send2, recv2):
     nx, nz, rows, width = out_ref.shape
+    groups = nsect * ny
+    slots = rows // groups
     quarter = width // 4
     c = lax.axis_index("sect")
     y = lax.axis_index("ey")
@@ -220,14 +222,38 @@
             return (c, y, mx, lax.rem(mz + d + nz, nz))
         return (c, y, lax.rem(mx + d + nx, nx), mz)
 
+    me_group = c * ny + y
+
+    def peer(o):
+        g = lax.rem(me_group + o, groups)
+        return (g // ny, lax.rem(g, ny), mx, mz)
+
     barrier = pltpu.get_barrier_semaphore()
     for axis in ("x", "z"):
         for d in (1, -1):
             pl.semaphore_signal(barrier, inc=1, device_id=dev(axis, d), device_id_type=MESH_ID)
-    pl.semaphore_wait(barrier, 4)
-
-    local = pltpu.make_async_copy(in_ref, out_ref.at[mx, mz], local_sem)
+    for o in range(1, groups):
+        pl.semaphore_signal(barrier, inc=1, device_id=peer(o), device_id_type=MESH_ID)
+    pl.semaphore_wait(barrier, 4 + groups - 1)
+
+    mine = pl.ds(pl.multiple_of(me_group * slots, slots), slots)
+    local = pltpu.make_async_copy(in_ref.at[me_group], out_ref.at[mx, mz, mine], local_sem)
     local.start()
+    dispatch = []
+    for o in range(1, groups):
+        cp = pltpu.make_async_remote_copy(
+            src_ref=in_ref.at[lax.rem(me_group + o, groups)],
+            dst_ref=out_ref.at[mx, mz, mine],
+            send_sem=in_send.at[o],
+            recv_sem=in_recv.at[o],
+            device_id=peer(o),
+            device_id_type=MESH_ID,
+        )
+        cp.start()
+        dispatch.append(cp)
+    local.wait()
+    for cp in dispatch:
+        cp.wait_recv()
 
     rings = [("z", 1), ("z", -1), ("x", 1), ("x", -1)]
 
@@ -275,9 +301,8 @@
         return copies
 
     copies1 = ring_phase(
-        lambda r: rings[r][0], block, lambda r: in_ref.at[:, cols(r)], send1, recv1, nz
-    )
-    local.wait()
+        lambda r: rings[r][0], block, lambda r: out_ref.at[mx, mz, :, cols(r)], send1, recv1, nz
+    )
 
     def second(r):
         return "x" if rings[r][0] == "z" else "z"
@@ -290,19 +315,22 @@
         recv2,
         nx,
     )
-    for cp in list(copies1.values()) + list(copies2.values()):
+    for cp in list(copies1.values()) + list(copies2.values()) + dispatch:
         cp.wait_send()
 
 
-def plane_all_gather(rows_block, nx, nz):
-    rows, width = rows_block.shape
+def plane_all_gather(slab, nx, nz, nsect, ny):
+    groups, slots, width = slab.shape
+    rows = groups * slots
     return pl.pallas_call(
-        ag_kernel,
-        out_shape=jax.ShapeDtypeStruct((nx, nz, rows, width), rows_block.dtype),
+        functools.partial(ag_kernel, nsect, ny),
+        out_shape=jax.ShapeDtypeStruct((nx, nz, rows, width), slab.dtype),
         in_specs=[pl.BlockSpec(memory_space=pltpu.VMEM)],
         out_specs=pl.BlockSpec(memory_space=pltpu.VMEM),
         scratch_shapes=[
             pltpu.SemaphoreType.DMA(()),
+            pltpu.SemaphoreType.DMA((groups,)),
+            pltpu.SemaphoreType.DMA((groups,)),
             pltpu.SemaphoreType.DMA((4, nz - 1)),
             pltpu.SemaphoreType.DMA((4, nz - 1)),
             pltpu.SemaphoreType.DMA((4, nx - 1)),
@@ -311,7 +339,7 @@
         compiler_params=pltpu.CompilerParams(
             collective_id=1, has_side_effects=True, vmem_limit_bytes=60 * 1024 * 1024
         ),
-    )(rows_block)
+    )(slab)
 
 
 ALL = ("sect", "ey", "ex", "tp")
@@ -342,10 +370,9 @@
     repeated = jnp.repeat(tokens, 2, axis=0)
     slab = jnp.dot(picker, repeated, preferred_element_type=jnp.float32).astype(jnp.bfloat16)
     slab = slab.reshape(experts_all, capacity, model_width)
-    column_rows = lax.all_to_all(slab, EXPERT_AXES, split_axis=0, concat_axis=0, tiled=True)
     nx = lax.axis_size("ex")
     plane_rows = plane_all_gather(
-        column_rows.reshape(experts_all * capacity, model_width), nx, plane_count // nx
+        slab, nx, plane_count // nx, lax.axis_size("sect"), lax.axis_size("ey")
     )
     expert_out = expert_reduce_scatter(
         plane_rows, w_gate[0], w_up[0], w_down[0], lax.axis_size("sect"), lax.axis_size("ey")

time: 150 us -> 149 us (level)
  Pallas kernels: 125 us -> 135 us
  starting transfers between devices: 5.97 us -> 0 us
  waiting for transfers between devices: 4.57 us -> 0 us
    pallas_call x1, Pallas kernels: 44.3 us -> 55.6 us  [plane_all_gather(): pl.pallas_call(functools.partial(ag_kernel, nsect, ny), out_shape=jax.Sha...]
    all_to_all x1 -> x0, starting transfers between devices: 5.97 us -> none  [per_device(): lax.all_to_all(slab, EXPERT_AXES, split_axis=0, concat_axis=0, tiled=True)]
    all_to_all x1 -> x0, waiting for transfers between devices: 4.57 us -> none  [per_device(): lax.all_to_all(slab, EXPERT_AXES, split_axis=0, concat_axis=0, tiled=True)]
  transfers between devices with their start and end apart: 1 -> 0, of which waited for: 1 -> 0; matrix products, arithmetic and copies ran while one was open for 2% -> 0% of each run, Pallas kernels for 0% -> 0%
where the time goes in v7:
time: 149 us; the launch traced here: 147 us
  Pallas kernels  135 us (91%)
  local copies, waits for them, and re-layouts  7.35 us (5%)
  other arithmetic  4.28 us (3%)
    pallas_call x1, Pallas kernels, expert_reduce_scatter(): pl.pallas_call(functools.partial(rs_kernel, nsect, ny), out_shape=jax.Sha...  79 us
    pallas_call x1, Pallas kernels, plane_all_gather(): pl.pallas_call(functools.partial(ag_kernel, nsect, ny), out_shape=jax.Sha...  55.6 us

profile of v7, /device:TPU:1, one launch (start us, length us, event | category | flops | bytes accessed | tf_op | source)
XLA Modules:
  0.0 146.5 jit_solution(7960348985722827861)
XLA Ops:
  0.0 0.8 copy.10
  0.8 0.0 copy-start
  0.8 0.1 reshape.66
  0.8 0.1 fusion.1
  0.9 0.2 select_reduce_fusion
  1.1 0.2 copy-done
  1.3 0.0 copy-start.1
  1.3 0.5 copy-done.1
  1.9 1.0 broadcast_in_dim.17
  2.9 0.1 reshape.67
  3.0 0.2 convolution_convert_fusion
  3.2 0.9 reshape.68.in_ref
  4.1 55.6 %shard_map.64.rows_ref = bf16[4,4,32,6144]{3,2,1,0:T(8,128)(2,1)} custom-call(bf16[8,4,6144]{2,1,0:T(4,128)(2,1)} %reshape.68.in_ref), custom_call_target="tpu_custom_call" | custom-call | tf_op jit(solution)/shard_map/pallas_call | solution.py:325
  59.7 79.0 %shard_map.65 = f32[32,6144]{1,0:T(8,128)} custom-call(bf16[4,4,32,6144]{3,2,1,0:T(8,128)(2,1)} %shard_map.64.rows_ref, bf16[6144,512]{1,0:T(8,128)(2,1)} %bitcast.10, bf16[6144,512]{1,0:T(8,128)(2,1)} %bitcast.11, bf16[512,6144]{1,0:T(8,128)(2,1)} %bitcast.12), custom_call_target="tpu_custom_call" | custom-call | tf_op jit(solution)/shard_map/pallas_call | solution.py:175
  138.7 0.7 broadcast_multiply_fusion
  139.4 0.1 mul.37
  139.5 0.6 fusion.2
  140.1 2.0 %gather_fusion = f32[16,6144]{1,0:T(8,128)S(1)} fusion(f32[32,6144]{1,0:T(8,128)} %shard_map.65, s32[1024]{0:T(1024)S(1)} %pad_clamp_fusion), kind=kCustom, calls=%fused_computation | custom fusion | bytes 786496 | tf_op jit(solution)/shard_map/jit(_take)/gather | solution.py:381
  142.1 0.2 gather.7
  142.4 0.7 reduce_sum.23
  143.1 0.7 compare_and_fusion
  143.8 0.7 rev.3
  144.5 0.7 add_divide_fusion
  145.2 0.1 copy.12
  145.2 1.3 multiply_reduce_fusion
  (3 shorter events, 0.0 us)
Async XLA Ops:
  0.8 0.6 copy-start
  1.3 0.5 copy-start.1

commit v8 on v7

--- a/solution.py
+++ b/solution.py
@@ -13,8 +13,8 @@
 
 
 def rs_kernel(
-    nsect, ny, rows_ref, wg_hbm, wu_hbm, wd_hbm, out_ref,
-    wg, wu, wd, hid, stage, fin, s1, total1, s2, wsem, send1, recv1, send2, recv2, local_sem, ret_send, ret_recv,
+    nsect, ny, col_ref, mix_w_ref, rows_ref, wg_hbm, wu_hbm, wd_hbm, mix_ref,
+    out_ref, wg, wu, wd, hid, stage, fin, s1, total1, s2, wsem, send1, recv1, send2, recv2, local_sem, ret_send, ret_recv,
 ):
     nx, nz, rows, width = rows_ref.shape
     hidden_width = wd.shape[0]
@@ -163,19 +163,26 @@
     local.wait()
     for cp in returns:
         cp.wait_recv()
+    for t in range(mix_ref.shape[0]):
+        first = out_ref[pl.ds(col_ref[2 * t], 1), :]
+        second = out_ref[pl.ds(col_ref[2 * t + 1], 1), :]
+        mix = mix_w_ref[2 * t] * first + mix_w_ref[2 * t + 1] * second
+        mix_ref[pl.ds(t, 1), :] = mix.astype(mix_ref.dtype)
     for cp in list(copies1.values()) + list(copies2.values()) + returns:
         cp.wait_send()
 
 
-def expert_reduce_scatter(expert_rows, w_gate, w_up, w_down, nsect, ny):
+def expert_reduce_scatter(columns, mix_w, expert_rows, w_gate, w_up, w_down, nsect, ny):
     nx, nz, rows, width = expert_rows.shape
     hidden_width = w_down.shape[0]
     quarter = width // 4
     groups = nsect * ny
     return pl.pallas_call(
         functools.partial(rs_kernel, nsect, ny),
-        out_shape=jax.ShapeDtypeStruct((rows, width), jnp.float32),
+        out_shape=jax.ShapeDtypeStruct((columns.shape[0] // 2, width), jnp.bfloat16),
         in_specs=[
+            pl.BlockSpec(memory_space=pltpu.SMEM),
+            pl.BlockSpec(memory_space=pltpu.SMEM),
             pl.BlockSpec(memory_space=pltpu.VMEM),
             pl.BlockSpec(memory_space=pl.ANY),
             pl.BlockSpec(memory_space=pl.ANY),
@@ -183,6 +190,7 @@
         ],
         out_specs=pl.BlockSpec(memory_space=pltpu.VMEM),
         scratch_shapes=[
+            pltpu.VMEM((rows, width), jnp.float32),
             pltpu.VMEM(w_gate.shape, w_gate.dtype),
             pltpu.VMEM(w_up.shape, w_up.dtype),
             pltpu.VMEM(w_down.shape, w_down.dtype),
@@ -204,7 +212,7 @@
         compiler_params=pltpu.CompilerParams(
             collective_id=0, has_side_effects=True, vmem_limit_bytes=64 * 1024 * 1024
         ),
-    )(expert_rows, w_gate, w_up, w_down)
+    )(columns, mix_w, expert_rows, w_gate, w_up, w_down)
 
 
 def ag_kernel(nsect, ny, in_ref, out_ref, local_sem, in_send, in_recv, send1, recv1, send2, recv2):
@@ -374,13 +382,17 @@
     plane_rows = plane_all_gather(
         slab, nx, plane_count // nx, lax.axis_size("sect"), lax.axis_size("ey")
     )
-    expert_out = expert_reduce_scatter(
-        plane_rows, w_gate[0], w_up[0], w_down[0], lax.axis_size("sect"), lax.axis_size("ey")
-    )
     weights = jax.nn.sigmoid(router_logits - router_logits[:, ::-1]).reshape(-1)
-    picked = jnp.take(expert_out, columns, axis=0) * weights[:, None]
-    mixture = jnp.sum(picked.reshape(token_count, 2, model_width), axis=1)
-    return mixture.astype(jnp.bfloat16)
+    return expert_reduce_scatter(
+        columns.astype(jnp.int32),
+        weights,
+        plane_rows,
+        w_gate[0],
+        w_up[0],
+        w_down[0],
+        lax.axis_size("sect"),
+        lax.axis_size("ey"),
+    )
 
 
 def x_extent(devices):

time: 149 us -> 142 us (0.953)
  other arithmetic: 4.28 us -> 0.31 us
  local copies, waits for them, and re-layouts: 7.35 us -> 5.17 us
    gather x2 -> x0, local copies, waits for them, and re-layouts: 2.21 us -> none  [per_device(): picked = jnp.take(expert_out, columns, axis=0) * weights[:, None]]
where the time goes in v8:
time: 142 us; the launch traced here: 141 us
  Pallas kernels  135 us (95%)
  local copies, waits for them, and re-layouts  5.17 us (4%)
    pallas_call x1, Pallas kernels, expert_reduce_scatter(): pl.pallas_call(functools.partial(rs_kernel, nsect, ny), out_shape=jax.Sha...  79.2 us
    pallas_call x1, Pallas kernels, plane_all_gather(): pl.pallas_call(functools.partial(ag_kernel, nsect, ny), out_shape=jax.Sha...  55.6 us

profile of v8, /device:TPU:1, one launch (start us, length us, event | category | flops | bytes accessed | tf_op | source)
XLA Modules:
  0.0 140.5 jit_solution(4343066217214827497)
XLA Ops:
  0.0 0.0 copy-start
  0.0 0.8 copy.9
  0.8 0.1 reshape.21
  0.9 0.1 fusion.1
  1.0 0.2 select_reduce_fusion
  1.2 0.0 copy-start.1
  1.2 1.0 broadcast_in_dim.2
  2.2 0.1 reshape.23
  2.3 0.2 convolution_convert_fusion
  2.5 0.9 reshape.24.in_ref
  3.4 55.6 %shard_map.64.rows_ref = bf16[4,4,32,6144]{3,2,1,0:T(8,128)(2,1)} custom-call(bf16[8,4,6144]{2,1,0:T(4,128)(2,1)} %reshape.24.in_ref), custom_call_target="tpu_custom_call" | custom-call | tf_op jit(solution)/shard_map/pallas_call | solution.py:333
  59.0 0.0 copy-done
  59.0 0.1 copy.10
  59.1 0.7 reshape.22.mix_w_ref
  59.8 0.0 copy-done.1
  59.8 79.2 %shard_map.65 = bf16[8,6144]{1,0:T(8,128)(2,1)} custom-call(s32[16]{0:T(128)} %copy-done.1, f32[16]{0:T(128)} %reshape.22.mix_w_ref, bf16[4,4,32,6144]{3,2,1,0:T(8,128)(2,1)} %shard_map.64.rows_ref, bf16[6144,512]{1,0:T(8,128)(2,1)} %bitcast.4, bf16[6144,512]{1,0:T(8,128)(2,1)} %bitcast.5, bf16[512,6144]{1,0:T(8,128)(2,1)} %bitcast.6), custom_call_target="tpu_custom_call" | custom-call | tf_op jit(solution)/shard_map/pallas_call | solution.py:180
  139.0 1.5 %copy.12 = bf16[8,6144]{1,0:T(8,128)(2,1)} copy(bf16[8,6144]{1,0:T(8,128)(2,1)} %shard_map.65) | data formatting | bytes 196608
  (4 shorter events, 0.1 us)
Async XLA Ops:
  0.0 59.0 %copy-start = (f32[8,2]{0,1:T(2,128)S(1)}, f32[8,2]{0,1:T(2,128)}, u32[]{:S(2)}) copy-start(f32[8,2]{0,1:T(2,128)} %param.7) | copy-start | bytes 196
  1.2 58.6 %copy-start.1 = (s32[16]{0:T(128)}, s32[16]{0:T(128)S(1)}, u32[]{:S(2)}) copy-start(s32[16]{0:T(128)S(1)} %multiply_add_fusion.col_ref) | copy-start | bytes 196

commit v9 on v8

--- a/solution.py
+++ b/solution.py
@@ -14,7 +14,7 @@
 
 def rs_kernel(
     nsect, ny, col_ref, mix_w_ref, rows_ref, wg_hbm, wu_hbm, wd_hbm, mix_ref,
-    out_ref, wg, wu, wd, hid, stage, fin, s1, total1, s2, wsem, send1, recv1, send2, recv2, local_sem, ret_send, ret_recv,
+    out_ref, wg, wu, wd, hid, stage, stage_f1, stage2_d, stage2_f, fin, s1, total1, s2, wsem, send1, recv1, send2, recv2, local_sem, ret_send, ret_recv,
 ):
     nx, nz, rows, width = rows_ref.shape
     hidden_width = wd.shape[0]
@@ -71,6 +71,9 @@
     def me_on(axis):
         return mz if axis == "z" else mx
 
+    def size_on(axis):
+        return nz if axis == "z" else nx
+
     def cols(r):
         return pl.ds(r * quarter, quarter)
 
@@ -88,61 +91,67 @@
     def other(axis):
         return "x" if axis == "z" else "z"
 
-    n1 = nz
-    copies1 = {}
-    for s in range(n1 - 1):
+    def both_sides(axis_of, own, stage_d, stage_f, recv_d, recv_f, recv_s, send, recv, finish):
+        copies = []
+        pending = {}
         for r in range(4):
-            axis, d = rings[r][0], rings[r][1]
-            j = lax.rem(me_on(axis) + n1 * (s + 2) - d * (s + 1), n1)
-            if s == 0:
-                stage[r] = chunk(r, j).astype(stage.dtype)
-                src = stage.at[r]
-            else:
-                part = chunk(r, j)
-                copies1[(r, s - 1)].wait_recv()
-                s1[r, s - 1] = (s1[r, s - 1].astype(jnp.float32) + part).astype(s1.dtype)
-                src = s1.at[r, s - 1]
-            cp = pltpu.make_async_remote_copy(
-                src_ref=src,
-                dst_ref=s1.at[r, s],
-                send_sem=send1.at[r, s],
-                recv_sem=recv1.at[r, s],
-                device_id=dev(axis, d),
-                device_id_type=MESH_ID,
+            axis, d = axis_of(r), rings[r][1]
+            n = size_on(axis)
+            me = me_on(axis)
+            stage_d[r] = own(r, lax.rem(me + n + d, n)).astype(stage_d.dtype)
+            direct = pltpu.make_async_remote_copy(
+                src_ref=stage_d.at[r], dst_ref=recv_d.at[r], send_sem=send.at[r, 0],
+                recv_sem=recv.at[r, 0], device_id=dev(axis, d), device_id_type=MESH_ID,
             )
-            cp.start()
-            copies1[(r, s)] = cp
-    for r in range(4):
-        part = chunk(r, me_on(rings[r][0]))
-        copies1[(r, n1 - 2)].wait_recv()
-        total1[r] = s1[r, n1 - 2].astype(jnp.float32) + part
-
-    n2 = nx
-    copies2 = {}
-    for s in range(n2 - 1):
+            direct.start()
+            stage_f[r] = own(r, lax.rem(me + 2 * n - 2 * d, n)).astype(stage_f.dtype)
+            forward = pltpu.make_async_remote_copy(
+                src_ref=stage_f.at[r], dst_ref=recv_f.at[r], send_sem=send.at[r, 1],
+                recv_sem=recv.at[r, 1], device_id=dev(axis, -d), device_id_type=MESH_ID,
+            )
+            forward.start()
+            pending[r] = (direct, forward)
+            copies += [direct, forward]
         for r in range(4):
-            axis, d = other(rings[r][0]), rings[r][1]
-            j = lax.rem(me_on(axis) + n2 * (s + 2) - d * (s + 1), n2)
-            if s == 0:
-                src = total1.at[r, j]
-            else:
-                copies2[(r, s - 1)].wait_recv()
-                s2[r, s - 1] += total1[r, j]
-                src = s2.at[r, s - 1]
-            cp = pltpu.make_async_remote_copy(
-                src_ref=src,
-                dst_ref=s2.at[r, s],
-                send_sem=send2.at[r, s],
-                recv_sem=recv2.at[r, s],
-                device_id=dev(axis, d),
-                device_id_type=MESH_ID,
+            axis, d = axis_of(r), rings[r][1]
+            n = size_on(axis)
+            me = me_on(axis)
+            term = own(r, lax.rem(me + n - d, n))
+            pending[r][1].wait_recv()
+            recv_f[r] = (recv_f[r].astype(jnp.float32) + term).astype(recv_f.dtype)
+            second = pltpu.make_async_remote_copy(
+                src_ref=recv_f.at[r], dst_ref=recv_s.at[r], send_sem=send.at[r, 2],
+                recv_sem=recv.at[r, 2], device_id=dev(axis, -d), device_id_type=MESH_ID,
             )
-            cp.start()
-            copies2[(r, s)] = cp
-    for r in range(4):
-        copies2[(r, n2 - 2)].wait_recv()
-        axis = other(rings[r][0])
-        fin[:, cols(r)] = s2[r, n2 - 2] + total1[r, me_on(axis)]
+            second.start()
+            pending[r] = (pending[r][0], second)
+            copies.append(second)
+        for r in range(4):
+            axis = axis_of(r)
+            term = own(r, me_on(axis))
+            pending[r][0].wait_recv()
+            pending[r][1].wait_recv()
+            finish(r, term + recv_d[r].astype(jnp.float32) + recv_s[r].astype(jnp.float32))
+        return copies
+
+    def keep_total1(r, value):
+        total1[r] = value
+
+    copies1 = both_sides(
+        lambda r: rings[r][0], chunk, stage, stage_f1, s1.at[:, 0], s1.at[:, 1], s1.at[:, 2],
+        send1, recv1, keep_total1,
+    )
+
+    def other_axis(r):
+        return other(rings[r][0])
+
+    def keep_fin(r, value):
+        fin[:, cols(r)] = value
+
+    copies2 = both_sides(
+        other_axis, lambda r, j: total1[r, j], stage2_d, stage2_f, s2.at[:, 0], s2.at[:, 1], s2.at[:, 2],
+        send2, recv2, keep_fin,
+    )
 
     mine = pl.ds(pl.multiple_of(me_group * slots, slots), slots)
     local = pltpu.make_async_copy(fin.at[mine], out_ref.at[mine], local_sem)
@@ -168,7 +177,7 @@
         second = out_ref[pl.ds(col_ref[2 * t + 1], 1), :]
         mix = mix_w_ref[2 * t] * first + mix_w_ref[2 * t + 1] * second
         mix_ref[pl.ds(t, 1), :] = mix.astype(mix_ref.dtype)
-    for cp in list(copies1.values()) + list(copies2.values()) + returns:
+    for cp in copies1 + copies2 + returns:
         cp.wait_send()
 
 
@@ -196,15 +205,18 @@
             pltpu.VMEM(w_down.shape, w_down.dtype),
             pltpu.VMEM((nx, nz, rows, hidden_width), jnp.bfloat16),
             pltpu.VMEM((4, nx, rows, quarter), jnp.bfloat16),
+            pltpu.VMEM((4, nx, rows, quarter), jnp.bfloat16),
+            pltpu.VMEM((4, rows, quarter), jnp.float32),
+            pltpu.VMEM((4, rows, quarter), jnp.float32),
             pltpu.VMEM((rows, width), jnp.float32),
-            pltpu.VMEM((4, nz - 1, nx, rows, quarter), jnp.bfloat16),
+            pltpu.VMEM((4, 3, nx, rows, quarter), jnp.bfloat16),
             pltpu.VMEM((4, nx, rows, quarter), jnp.float32),
-            pltpu.VMEM((4, nx - 1, rows, quarter), jnp.float32),
+            pltpu.VMEM((4, 3, rows, quarter), jnp.float32),
             pltpu.SemaphoreType.DMA((3,)),
-            pltpu.SemaphoreType.DMA((4, nz - 1)),
-            pltpu.SemaphoreType.DMA((4, nz - 1)),
-            pltpu.SemaphoreType.DMA((4, nx - 1)),
-            pltpu.SemaphoreType.DMA((4, nx - 1)),
+            pltpu.SemaphoreType.DMA((4, 3)),
+            pltpu.SemaphoreType.DMA((4, 3)),
+            pltpu.SemaphoreType.DMA((4, 3)),
+            pltpu.SemaphoreType.DMA((4, 3)),
             pltpu.SemaphoreType.DMA(()),
             pltpu.SemaphoreType.DMA((groups,)),
             pltpu.SemaphoreType.DMA((groups,)),

time: 142 us -> 137 us (0.965)
  Pallas kernels: 135 us -> 130 us
    pallas_call x1, Pallas kernels: 79.2 us -> 74.4 us  [expert_reduce_scatter(): pl.pallas_call(functools.partial(rs_kernel, nsect, ny), out_shape=jax.Sha...]
where the time goes in v9:
time: 137 us; the launch traced here: 136 us
  Pallas kernels  130 us (95%)
  local copies, waits for them, and re-layouts  5.17 us (4%)
    pallas_call x1, Pallas kernels, expert_reduce_scatter(): pl.pallas_call(functools.partial(rs_kernel, nsect, ny), out_shape=jax.Sha...  74.4 us
    pallas_call x1, Pallas kernels, plane_all_gather(): pl.pallas_call(functools.partial(ag_kernel, nsect, ny), out_shape=jax.Sha...  55.6 us

profile of v9, /device:TPU:1, one launch (start us, length us, event | category | flops | bytes accessed | tf_op | source)
XLA Modules:
  0.0 135.7 jit_solution(1140991742222914999)
XLA Ops:
  0.0 0.0 copy-start
  0.0 0.8 copy.9
  0.8 0.1 reshape.21
  0.9 0.1 fusion.1
  1.0 0.2 select_reduce_fusion
  1.2 0.0 copy-start.1
  1.2 1.0 broadcast_in_dim.2
  2.2 0.1 reshape.23
  2.3 0.2 convolution_convert_fusion
  2.5 0.9 reshape.24.in_ref
  3.4 55.6 %shard_map.64.rows_ref = bf16[4,4,32,6144]{3,2,1,0:T(8,128)(2,1)} custom-call(bf16[8,4,6144]{2,1,0:T(4,128)(2,1)} %reshape.24.in_ref), custom_call_target="tpu_custom_call" | custom-call | tf_op jit(solution)/shard_map/pallas_call | solution.py:345
  59.0 0.0 copy-done
  59.0 0.1 copy.10
  59.1 0.7 reshape.22.mix_w_ref
  59.8 0.0 copy-done.1
  59.8 74.4 %shard_map.65 = bf16[8,6144]{1,0:T(8,128)(2,1)} custom-call(s32[16]{0:T(128)} %copy-done.1, f32[16]{0:T(128)} %reshape.22.mix_w_ref, bf16[4,4,32,6144]{3,2,1,0:T(8,128)(2,1)} %shard_map.64.rows_ref, bf16[6144,512]{1,0:T(8,128)(2,1)} %bitcast.4, bf16[6144,512]{1,0:T(8,128)(2,1)} %bitcast.5, bf16[512,6144]{1,0:T(8,128)(2,1)} %bitcast.6), custom_call_target="tpu_custom_call" | custom-call | tf_op jit(solution)/shard_map/pallas_call | solution.py:189
  134.2 1.5 %copy.12 = bf16[8,6144]{1,0:T(8,128)(2,1)} copy(bf16[8,6144]{1,0:T(8,128)(2,1)} %shard_map.65) | data formatting | bytes 196608
  (4 shorter events, 0.1 us)
Async XLA Ops:
  0.0 59.0 %copy-start = (f32[8,2]{0,1:T(2,128)S(1)}, f32[8,2]{0,1:T(2,128)}, u32[]{:S(2)}) copy-start(f32[8,2]{0,1:T(2,128)} %param.7) | copy-start | bytes 196
  1.2 58.6 %copy-start.1 = (s32[16]{0:T(128)}, s32[16]{0:T(128)S(1)}, u32[]{:S(2)}) copy-start(s32[16]{0:T(128)S(1)} %multiply_add_fusion.col_ref) | copy-start | bytes 196

commit v10 on v9

--- a/solution.py
+++ b/solution.py
@@ -293,49 +293,46 @@
     def me_on(axis):
         return mz if axis == "z" else mx
 
-    def ring_phase(axis_of, view, first_src, send, recv, sizes):
-        copies = {}
-        n = sizes
-        for s in range(n - 1):
-            for r in range(4):
-                axis, d = axis_of(r), rings[r][1]
-                me = me_on(axis)
-                k = lax.rem(me + n * (s + 1) - d * s, n)
-                if s == 0:
-                    src = first_src(r)
-                else:
-                    copies[(r, s - 1)].wait_recv()
-                    src = view(axis, r, k)
+    def both_sides(axis_of, view, send, recv):
+        copies = []
+        first = {}
+        for r in range(4):
+            axis, d = axis_of(r), rings[r][1]
+            me = me_on(axis)
+            src = view(axis, r, me)
+            for side, sign in ((0, d), (1, -d)):
                 cp = pltpu.make_async_remote_copy(
-                    src_ref=src,
-                    dst_ref=view(axis, r, k),
-                    send_sem=send.at[r, s],
-                    recv_sem=recv.at[r, s],
-                    device_id=dev(axis, d),
-                    device_id_type=MESH_ID,
+                    src_ref=src, dst_ref=src, send_sem=send.at[r, side], recv_sem=recv.at[r, side],
+                    device_id=dev(axis, sign), device_id_type=MESH_ID,
                 )
                 cp.start()
-                copies[(r, s)] = cp
-        for r in range(4):
-            copies[(r, n - 2)].wait_recv()
+                first[(r, side)] = cp
+                copies.append(cp)
+        later = {}
+        for r in range(4):
+            axis, d = axis_of(r), rings[r][1]
+            n = nz if axis == "z" else nx
+            first[(r, 1)].wait_recv()
+            passing = view(axis, r, lax.rem(me_on(axis) + n + d, n))
+            cp = pltpu.make_async_remote_copy(
+                src_ref=passing, dst_ref=passing, send_sem=send.at[r, 2], recv_sem=recv.at[r, 2],
+                device_id=dev(axis, -d), device_id_type=MESH_ID,
+            )
+            cp.start()
+            later[r] = cp
+            copies.append(cp)
+        for r in range(4):
+            first[(r, 0)].wait_recv()
+            later[r].wait_recv()
         return copies
 
-    copies1 = ring_phase(
-        lambda r: rings[r][0], block, lambda r: out_ref.at[mx, mz, :, cols(r)], send1, recv1, nz
-    )
+    copies1 = both_sides(lambda r: rings[r][0], block, send1, recv1)
 
     def second(r):
         return "x" if rings[r][0] == "z" else "z"
 
-    copies2 = ring_phase(
-        second,
-        plane_block,
-        lambda r: plane_block(second(r), r, me_on(second(r))),
-        send2,
-        recv2,
-        nx,
-    )
-    for cp in list(copies1.values()) + list(copies2.values()) + dispatch:
+    copies2 = both_sides(second, plane_block, send2, recv2)
+    for cp in copies1 + copies2 + dispatch:
         cp.wait_send()
 
 
@@ -351,10 +348,10 @@
             pltpu.SemaphoreType.DMA(()),
             pltpu.SemaphoreType.DMA((groups,)),
             pltpu.SemaphoreType.DMA((groups,)),
-            pltpu.SemaphoreType.DMA((4, nz - 1)),
-            pltpu.SemaphoreType.DMA((4, nz - 1)),
-            pltpu.SemaphoreType.DMA((4, nx - 1)),
-            pltpu.SemaphoreType.DMA((4, nx - 1)),
+            pltpu.SemaphoreType.DMA((4, 3)),
+            pltpu.SemaphoreType.DMA((4, 3)),
+            pltpu.SemaphoreType.DMA((4, 3)),
+            pltpu.SemaphoreType.DMA((4, 3)),
         ],
         compiler_params=pltpu.CompilerParams(
             collective_id=1, has_side_effects=True, vmem_limit_bytes=60 * 1024 * 1024

time: 137 us -> 131 us (0.956)
  Pallas kernels: 130 us -> 124 us
    pallas_call x1, Pallas kernels: 55.6 us -> 50.4 us  [plane_all_gather(): pl.pallas_call(functools.partial(ag_kernel, nsect, ny), out_shape=jax.Sha...]
where the time goes in v10:
time: 131 us; the launch traced here: 129 us
  Pallas kernels  124 us (95%)
  local copies, waits for them, and re-layouts  5.17 us (4%)
    pallas_call x1, Pallas kernels, expert_reduce_scatter(): pl.pallas_call(functools.partial(rs_kernel, nsect, ny), out_shape=jax.Sha...  73.3 us
    pallas_call x1, Pallas kernels, plane_all_gather(): pl.pallas_call(functools.partial(ag_kernel, nsect, ny), out_shape=jax.Sha...  50.4 us

profile of v10, /device:TPU:1, one launch (start us, length us, event | category | flops | bytes accessed | tf_op | source)
XLA Modules:
  0.0 129.4 jit_solution(5840381359523033534)
XLA Ops:
  0.0 0.0 copy-start
  0.0 0.8 copy.9
  0.8 0.1 reshape.21
  0.9 0.1 fusion.1
  1.0 0.2 select_reduce_fusion
  1.2 0.0 copy-start.1
  1.2 1.0 broadcast_in_dim.2
  2.2 0.1 reshape.23
  2.3 0.2 convolution_convert_fusion
  2.5 0.9 reshape.24.in_ref
  3.4 50.4 %shard_map.64.rows_ref = bf16[4,4,32,6144]{3,2,1,0:T(8,128)(2,1)} custom-call(bf16[8,4,6144]{2,1,0:T(4,128)(2,1)} %reshape.24.in_ref), custom_call_target="tpu_custom_call" | custom-call | tf_op jit(solution)/shard_map/pallas_call | solution.py:342
  53.8 0.0 copy-done
  53.8 0.1 copy.10
  53.9 0.7 reshape.22.mix_w_ref
  54.6 0.0 copy-done.1
  54.6 73.3 %shard_map.65 = bf16[8,6144]{1,0:T(8,128)(2,1)} custom-call(s32[16]{0:T(128)} %copy-done.1, f32[16]{0:T(128)} %reshape.22.mix_w_ref, bf16[4,4,32,6144]{3,2,1,0:T(8,128)(2,1)} %shard_map.64.rows_ref, bf16[6144,512]{1,0:T(8,128)(2,1)} %bitcast.4, bf16[6144,512]{1,0:T(8,128)(2,1)} %bitcast.5, bf16[512,6144]{1,0:T(8,128)(2,1)} %bitcast.6), custom_call_target="tpu_custom_call" | custom-call | tf_op jit(solution)/shard_map/pallas_call | solution.py:189
  127.9 1.5 %copy.12 = bf16[8,6144]{1,0:T(8,128)(2,1)} copy(bf16[8,6144]{1,0:T(8,128)(2,1)} %shard_map.65) | data formatting | bytes 196608
  (4 shorter events, 0.1 us)
Async XLA Ops:
  0.0 53.8 %copy-start = (f32[8,2]{0,1:T(2,128)S(1)}, f32[8,2]{0,1:T(2,128)}, u32[]{:S(2)}) copy-start(f32[8,2]{0,1:T(2,128)} %param.7) | copy-start | bytes 196
  1.2 53.4 %copy-start.1 = (s32[16]{0:T(128)}, s32[16]{0:T(128)S(1)}, u32[]{:S(2)}) copy-start(s32[16]{0:T(128)S(1)} %multiply_add_fusion.col_ref) | copy-start | bytes 196

commit v11 on v10

--- a/solution.py
+++ b/solution.py
@@ -13,8 +13,9 @@
 
 
 def rs_kernel(
-    nsect, ny, col_ref, mix_w_ref, rows_ref, wg_hbm, wu_hbm, wd_hbm, mix_ref,
+    nsect, ny, col_ref, mix_w_ref, slab_ref, wg_hbm, wu_hbm, wd_hbm, mix_ref,
     out_ref, wg, wu, wd, hid, stage, stage_f1, stage2_d, stage2_f, fin, s1, total1, s2, wsem, send1, recv1, send2, recv2, local_sem, ret_send, ret_recv,
+    rows_ref, g_local, g_in_send, g_in_recv, g_send1, g_recv1, g_send2, g_recv2,
 ):
     nx, nz, rows, width = rows_ref.shape
     hidden_width = wd.shape[0]
@@ -52,6 +53,9 @@
         pl.semaphore_signal(barrier, inc=1, device_id=peer(o), device_id_type=MESH_ID)
     pl.semaphore_wait(barrier, 4 + groups - 1)
 
+    gather_body(
+        nsect, ny, slab_ref, rows_ref, g_local, g_in_send, g_in_recv, g_send1, g_recv1, g_send2, g_recv2
+    )
     weight_copies[0].wait()
     weight_copies[1].wait()
 
@@ -181,11 +185,11 @@
         cp.wait_send()
 
 
-def expert_reduce_scatter(columns, mix_w, expert_rows, w_gate, w_up, w_down, nsect, ny):
-    nx, nz, rows, width = expert_rows.shape
+def expert_reduce_scatter(columns, mix_w, slab, w_gate, w_up, w_down, nsect, ny, nx, nz):
+    groups, slots, width = slab.shape
+    rows = groups * slots
     hidden_width = w_down.shape[0]
     quarter = width // 4
-    groups = nsect * ny
     return pl.pallas_call(
         functools.partial(rs_kernel, nsect, ny),
         out_shape=jax.ShapeDtypeStruct((columns.shape[0] // 2, width), jnp.bfloat16),
@@ -220,14 +224,22 @@
             pltpu.SemaphoreType.DMA(()),
             pltpu.SemaphoreType.DMA((groups,)),
             pltpu.SemaphoreType.DMA((groups,)),
+            pltpu.VMEM((nx, nz, rows, width), slab.dtype),
+            pltpu.SemaphoreType.DMA(()),
+            pltpu.SemaphoreType.DMA((groups,)),
+            pltpu.SemaphoreType.DMA((groups,)),
+            pltpu.SemaphoreType.DMA((4, 3)),
+            pltpu.SemaphoreType.DMA((4, 3)),
+            pltpu.SemaphoreType.DMA((4, 3)),
+            pltpu.SemaphoreType.DMA((4, 3)),
         ],
         compiler_params=pltpu.CompilerParams(
             collective_id=0, has_side_effects=True, vmem_limit_bytes=64 * 1024 * 1024
         ),
-    )(columns, mix_w, expert_rows, w_gate, w_up, w_down)
-
-
-def ag_kernel(nsect, ny, in_ref, out_ref, local_sem, in_send, in_recv, send1, recv1, send2, recv2):
+    )(columns, mix_w, slab, w_gate, w_up, w_down)
+
+
+def gather_body(nsect, ny, in_ref, out_ref, local_sem, in_send, in_recv, send1, recv1, send2, recv2):
     nx, nz, rows, width = out_ref.shape
     groups = nsect * ny
     slots = rows // groups
@@ -247,14 +259,6 @@
     def peer(o):
         g = lax.rem(me_group + o, groups)
         return (g // ny, lax.rem(g, ny), mx, mz)
-
-    barrier = pltpu.get_barrier_semaphore()
-    for axis in ("x", "z"):
-        for d in (1, -1):
-            pl.semaphore_signal(barrier, inc=1, device_id=dev(axis, d), device_id_type=MESH_ID)
-    for o in range(1, groups):
-        pl.semaphore_signal(barrier, inc=1, device_id=peer(o), device_id_type=MESH_ID)
-    pl.semaphore_wait(barrier, 4 + groups - 1)
 
     mine = pl.ds(pl.multiple_of(me_group * slots, slots), slots)
     local = pltpu.make_async_copy(in_ref.at[me_group], out_ref.at[mx, mz, mine], local_sem)
@@ -336,29 +340,6 @@
         cp.wait_send()
 
 
-def plane_all_gather(slab, nx, nz, nsect, ny):
-    groups, slots, width = slab.shape
-    rows = groups * slots
-    return pl.pallas_call(
-        functools.partial(ag_kernel, nsect, ny),
-        out_shape=jax.ShapeDtypeStruct((nx, nz, rows, width), slab.dtype),
-        in_specs=[pl.BlockSpec(memory_space=pltpu.VMEM)],
-        out_specs=pl.BlockSpec(memory_space=pltpu.VMEM),
-        scratch_shapes=[
-            pltpu.SemaphoreType.DMA(()),
-            pltpu.SemaphoreType.DMA((groups,)),
-            pltpu.SemaphoreType.DMA((groups,)),
-            pltpu.SemaphoreType.DMA((4, 3)),
-            pltpu.SemaphoreType.DMA((4, 3)),
-            pltpu.SemaphoreType.DMA((4, 3)),
-            pltpu.SemaphoreType.DMA((4, 3)),
-        ],
-        compiler_params=pltpu.CompilerParams(
-            collective_id=1, has_side_effects=True, vmem_limit_bytes=60 * 1024 * 1024
-        ),
-    )(slab)
-
-
 ALL = ("sect", "ey", "ex", "tp")
 EXPERT_AXES = ("sect", "ey")
 PLANE_AXES = ("ex", "tp")
@@ -388,19 +369,18 @@
     slab = jnp.dot(picker, repeated, preferred_element_type=jnp.float32).astype(jnp.bfloat16)
     slab = slab.reshape(experts_all, capacity, model_width)
     nx = lax.axis_size("ex")
-    plane_rows = plane_all_gather(
-        slab, nx, plane_count // nx, lax.axis_size("sect"), lax.axis_size("ey")
-    )
     weights = jax.nn.sigmoid(router_logits - router_logits[:, ::-1]).reshape(-1)
     return expert_reduce_scatter(
         columns.astype(jnp.int32),
         weights,
-        plane_rows,
+        slab,
         w_gate[0],
         w_up[0],
         w_down[0],
         lax.axis_size("sect"),
         lax.axis_size("ey"),
+        nx,
+        plane_count // nx,
     )
 
 

time: 131 us -> 123 us (0.939)
  Pallas kernels: 124 us -> 114 us
    pallas_call x1 -> x0, Pallas kernels: 50.4 us -> none  [plane_all_gather(): pl.pallas_call(functools.partial(ag_kernel, nsect, ny), out_shape=jax.Sha...]
    pallas_call x1, Pallas kernels: 73.3 us -> 114 us  [expert_reduce_scatter(): pl.pallas_call(functools.partial(rs_kernel, nsect, ny), out_shape=jax.Sha...]
where the time goes in v11:
time: 123 us; the launch traced here: 121 us
  Pallas kernels  114 us (93%)
  local copies, waits for them, and re-layouts  5.75 us (5%)
    pallas_call x1, Pallas kernels, expert_reduce_scatter(): pl.pallas_call(functools.partial(rs_kernel, nsect, ny), out_shape=jax.Sha...  114 us

profile of v11, /device:TPU:1, one launch (start us, length us, event | category | flops | bytes accessed | tf_op | source)
XLA Modules:
  0.0 121.0 jit_solution(9296968608120117664)
XLA Ops:
  0.0 0.8 copy.9
  0.8 0.1 reshape.21
  0.8 0.1 fusion.1
  0.9 0.2 select_reduce_fusion
  1.1 0.0 copy-start
  1.2 1.0 broadcast_in_dim.2
  2.2 0.1 reshape.23
  2.2 0.2 convolution_convert_fusion
  2.5 0.9 reshape.24.slab_ref
  3.4 0.7 rev.3
  4.1 0.7 add_divide_fusion
  4.8 0.1 copy.10
  4.8 0.6 reshape.22.mix_w_ref
  5.5 0.0 copy-done
  5.5 114.0 %shard_map.64 = bf16[8,6144]{1,0:T(8,128)(2,1)} custom-call(s32[16]{0:T(128)} %copy-done, f32[16]{0:T(128)} %reshape.22.mix_w_ref, bf16[8,4,6144]{2,1,0:T(4,128)(2,1)} %reshape.24.slab_ref, bf16[6144,512]{1,0:T(8,128)(2,1)} %bitcast.4, bf16[6144,512]{1,0:T(8,128)(2,1)} %bitcast.5, bf16[512,6144]{1,0:T(8,128)(2,1)} %bitcast.6), custom_call_target="tpu_custom_call" | custom-call | tf_op jit(solution)/shard_map/pallas_call | solution.py:193
  119.5 1.5 %copy.12 = bf16[8,6144]{1,0:T(8,128)(2,1)} copy(bf16[8,6144]{1,0:T(8,128)(2,1)} %shard_map.64) | data formatting | bytes 196608
  (2 shorter events, 0.0 us)
Async XLA Ops:
  1.1 4.3 %copy-start = (s32[16]{0:T(128)}, s32[16]{0:T(128)S(1)}, u32[]{:S(2)}) copy-start(s32[16]{0:T(128)S(1)} %multiply_add_fusion.col_ref) | copy-start | bytes 196

commit v12 on v11

--- a/solution.py
+++ b/solution.py
@@ -13,7 +13,7 @@
 
 
 def rs_kernel(
-    nsect, ny, col_ref, mix_w_ref, slab_ref, wg_hbm, wu_hbm, wd_hbm, mix_ref,
+    nsect, ny, col_ref, logits_ref, slab_ref, wg_hbm, wu_hbm, wd_hbm, mix_ref,
     out_ref, wg, wu, wd, hid, stage, stage_f1, stage2_d, stage2_f, fin, s1, total1, s2, wsem, send1, recv1, send2, recv2, local_sem, ret_send, ret_recv,
     rows_ref, g_local, g_in_send, g_in_recv, g_send1, g_recv1, g_send2, g_recv2,
 ):
@@ -176,18 +176,22 @@
     local.wait()
     for cp in returns:
         cp.wait_recv()
+    logits = logits_ref[...]
+    gap = logits[:, 1:2] - logits[:, 0:1]
+    w_first = 1.0 / (1.0 + jnp.exp(gap))
+    w_second = 1.0 / (1.0 + jnp.exp(-gap))
     for t in range(mix_ref.shape[0]):
         first = out_ref[pl.ds(col_ref[2 * t], 1), :]
         second = out_ref[pl.ds(col_ref[2 * t + 1], 1), :]
-        mix = mix_w_ref[2 * t] * first + mix_w_ref[2 * t + 1] * second
+        mix = w_first[t : t + 1] * first + w_second[t : t + 1] * second
         mix_ref[pl.ds(t, 1), :] = mix.astype(mix_ref.dtype)
     for cp in copies1 + copies2 + returns:
         cp.wait_send()
 
 
-def expert_reduce_scatter(columns, mix_w, slab, w_gate, w_up, w_down, nsect, ny, nx, nz):
-    groups, slots, width = slab.shape
-    rows = groups * slots
+def expert_reduce_scatter(columns, logits, slab, w_gate, w_up, w_down, nsect, ny, nx, nz):
+    rows, width = slab.shape
+    groups = nsect * ny
     hidden_width = w_down.shape[0]
     quarter = width // 4
     return pl.pallas_call(
@@ -195,7 +199,7 @@
         out_shape=jax.ShapeDtypeStruct((columns.shape[0] // 2, width), jnp.bfloat16),
         in_specs=[
             pl.BlockSpec(memory_space=pltpu.SMEM),
-            pl.BlockSpec(memory_space=pltpu.SMEM),
+            pl.BlockSpec(memory_space=pltpu.VMEM),
             pl.BlockSpec(memory_space=pltpu.VMEM),
             pl.BlockSpec(memory_space=pl.ANY),
             pl.BlockSpec(memory_space=pl.ANY),
@@ -236,7 +240,7 @@
         compiler_params=pltpu.CompilerParams(
             collective_id=0, has_side_effects=True, vmem_limit_bytes=64 * 1024 * 1024
         ),
-    )(columns, mix_w, slab, w_gate, w_up, w_down)
+    )(columns, logits, slab, w_gate, w_up, w_down)
 
 
 def gather_body(nsect, ny, in_ref, out_ref, local_sem, in_send, in_recv, send1, recv1, send2, recv2):
@@ -261,12 +265,12 @@
         return (g // ny, lax.rem(g, ny), mx, mz)
 
     mine = pl.ds(pl.multiple_of(me_group * slots, slots), slots)
-    local = pltpu.make_async_copy(in_ref.at[me_group], out_ref.at[mx, mz, mine], local_sem)
+    local = pltpu.make_async_copy(in_ref.at[mine], out_ref.at[mx, mz, mine], local_sem)
     local.start()
     dispatch = []
     for o in range(1, groups):
         cp = pltpu.make_async_remote_copy(
-            src_ref=in_ref.at[lax.rem(me_group + o, groups)],
+            src_ref=in_ref.at[pl.ds(pl.multiple_of(lax.rem(me_group + o, groups) * slots, slots), slots)],
             dst_ref=out_ref.at[mx, mz, mine],
             send_sem=in_send.at[o],
             recv_sem=in_recv.at[o],
@@ -367,12 +371,10 @@
     picker = (positions[:, None] == columns[None, :]).astype(jnp.bfloat16)
     repeated = jnp.repeat(tokens, 2, axis=0)
     slab = jnp.dot(picker, repeated, preferred_element_type=jnp.float32).astype(jnp.bfloat16)
-    slab = slab.reshape(experts_all, capacity, model_width)
     nx = lax.axis_size("ex")
-    weights = jax.nn.sigmoid(router_logits - router_logits[:, ::-1]).reshape(-1)
     return expert_reduce_scatter(
         columns.astype(jnp.int32),
-        weights,
+        router_logits,
         slab,
         w_gate[0],
         w_up[0],

time: 123 us -> 122 us (level)
    reshape x2 -> x0, local copies, waits for them, and re-layouts: 1.51 us -> none  [the longest x1 0.89 us: per_device(): slab = slab.reshape(experts_all, capacity, model_width)]
    unnamed x4 -> x5, local copies, waits for them, and re-layouts: 2.3 us -> 3.64 us
where the time goes in v12:
time: 122 us; the launch traced here: 120 us
  Pallas kernels  114 us (93%)
  local copies, waits for them, and re-layouts  4.8 us (4%)
    pallas_call x1, Pallas kernels, expert_reduce_scatter(): pl.pallas_call(functools.partial(rs_kernel, nsect, ny), out_shape=jax.Sha...  114 us
    unnamed x5, local copies, waits for them, and re-layouts  3.64 us

profile of v12, /device:TPU:1, one launch (start us, length us, event | category | flops | bytes accessed | tf_op | source)
XLA Modules:
  0.0 120.4 jit_solution(7415641169425240922)
XLA Ops:
  0.0 0.8 copy.9
  0.8 0.1 reshape.15
  0.8 0.1 fusion.1
  0.9 0.2 select_reduce_fusion
  1.1 0.0 copy-start
  1.2 1.0 broadcast_in_dim.2
  2.2 0.1 reshape.16
  2.2 1.0 convolution_convert_fusion.slab_ref
  3.2 0.0 copy-done
  3.2 1.3 %copy.10.logits_ref = f32[8,2]{1,0:T(8,128)} copy(f32[8,2]{0,1:T(2,128)} %param.7) | data formatting | bytes 128 | tf_op args[1]
  4.6 114.3 %shard_map.64 = bf16[8,6144]{1,0:T(8,128)(2,1)} custom-call(s32[16]{0:T(128)} %copy-done, f32[8,2]{1,0:T(8,128)} %copy.10.logits_ref, bf16[32,6144]{1,0:T(8,128)(2,1)} %convolution_convert_fusion.slab_ref, bf16[6144,512]{1,0:T(8,128)(2,1)} %bitcast.4, bf16[6144,512]{1,0:T(8,128)(2,1)} %bitcast.5, bf16[512,6144]{1,0:T(8,128)(2,1)} %bitcast.6), custom_call_target="tpu_custom_call" | custom-call | tf_op jit(solution)/shard_map/pallas_call | solution.py:197
  118.9 1.5 %copy.12 = bf16[8,6144]{1,0:T(8,128)(2,1)} copy(bf16[8,6144]{1,0:T(8,128)(2,1)} %shard_map.64) | data formatting | bytes 196608
  (2 shorter events, 0.0 us)
Async XLA Ops:
  1.1 2.1 %copy-start = (s32[16]{0:T(128)}, s32[16]{0:T(128)S(1)}, u32[]{:S(2)}) copy-start(s32[16]{0:T(128)S(1)} %multiply_add_fusion.col_ref) | copy-start | bytes 196

commit v13 on v12

--- a/solution.py
+++ b/solution.py
@@ -149,31 +149,35 @@
     def other_axis(r):
         return other(rings[r][0])
 
+    mine = pl.ds(pl.multiple_of(me_group * slots, slots), slots)
+    returns = []
+    locals_ = []
+
     def keep_fin(r, value):
         fin[:, cols(r)] = value
+        local = pltpu.make_async_copy(fin.at[mine, cols(r)], out_ref.at[mine, cols(r)], local_sem.at[r])
+        local.start()
+        locals_.append(local)
+        for o in range(1, groups):
+            g = lax.rem(me_group + o, groups)
+            cp = pltpu.make_async_remote_copy(
+                src_ref=fin.at[pl.ds(pl.multiple_of(g * slots, slots), slots), cols(r)],
+                dst_ref=out_ref.at[mine, cols(r)],
+                send_sem=ret_send.at[o, r],
+                recv_sem=ret_recv.at[o, r],
+                device_id=peer(o),
+                device_id_type=MESH_ID,
+            )
+            cp.start()
+            returns.append(cp)
 
     copies2 = both_sides(
         other_axis, lambda r, j: total1[r, j], stage2_d, stage2_f, s2.at[:, 0], s2.at[:, 1], s2.at[:, 2],
         send2, recv2, keep_fin,
     )
 
-    mine = pl.ds(pl.multiple_of(me_group * slots, slots), slots)
-    local = pltpu.make_async_copy(fin.at[mine], out_ref.at[mine], local_sem)
-    local.start()
-    returns = []
-    for o in range(1, groups):
-        g = lax.rem(me_group + o, groups)
-        cp = pltpu.make_async_remote_copy(
-            src_ref=fin.at[pl.ds(pl.multiple_of(g * slots, slots), slots)],
-            dst_ref=out_ref.at[mine],
-            send_sem=ret_send.at[o],
-            recv_sem=ret_recv.at[o],
-            device_id=peer(o),
-            device_id_type=MESH_ID,
-        )
-        cp.start()
-        returns.append(cp)
-    local.wait()
+    for local in locals_:
+        local.wait()
     for cp in returns:
         cp.wait_recv()
     logits = logits_ref[...]
@@ -225,9 +229,9 @@
             pltpu.SemaphoreType.DMA((4, 3)),
             pltpu.SemaphoreType.DMA((4, 3)),
             pltpu.SemaphoreType.DMA((4, 3)),
-            pltpu.SemaphoreType.DMA(()),
-            pltpu.SemaphoreType.DMA((groups,)),
-            pltpu.SemaphoreType.DMA((groups,)),
+            pltpu.SemaphoreType.DMA((4,)),
+            pltpu.SemaphoreType.DMA((groups, 4)),
+            pltpu.SemaphoreType.DMA((groups, 4)),
             pltpu.VMEM((nx, nz, rows, width), slab.dtype),
             pltpu.SemaphoreType.DMA(()),
             pltpu.SemaphoreType.DMA((groups,)),

time: 122 us -> 120 us (0.984); the launches traced: 120 us -> 120 us
  no operation moved by 1% of the time
where the time goes in v13:
time: 120 us
  Pallas kernels  114 us (95%)
  local copies, waits for them, and re-layouts  4.8 us (4%)
    pallas_call x1, Pallas kernels, expert_reduce_scatter(): pl.pallas_call(functools.partial(rs_kernel, nsect, ny), out_shape=jax.Sha...  114 us
    unnamed x5, local copies, waits for them, and re-layouts  3.64 us

profile of v13, /device:TPU:1, one launch (start us, length us, event | category | flops | bytes accessed | tf_op | source)
XLA Modules:
  0.0 120.1 jit_solution(2931190912336140682)
XLA Ops:
  0.0 0.8 copy.9
  0.8 0.1 reshape.15
  0.8 0.1 fusion.1
  0.9 0.2 select_reduce_fusion
  1.1 0.0 copy-start
  1.2 1.0 broadcast_in_dim.2
  2.2 0.1 reshape.16
  2.2 1.0 convolution_convert_fusion.slab_ref
  3.2 0.0 copy-done
  3.2 1.3 %copy.10.logits_ref = f32[8,2]{1,0:T(8,128)} copy(f32[8,2]{0,1:T(2,128)} %param.7) | data formatting | bytes 128 | tf_op args[1]
  4.6 114.0 %shard_map.64 = bf16[8,6144]{1,0:T(8,128)(2,1)} custom-call(s32[16]{0:T(128)} %copy-done, f32[8,2]{1,0:T(8,128)} %copy.10.logits_ref, bf16[32,6144]{1,0:T(8,128)(2,1)} %convolution_convert_fusion.slab_ref, bf16[6144,512]{1,0:T(8,128)(2,1)} %bitcast.4, bf16[6144,512]{1,0:T(8,128)(2,1)} %bitcast.5, bf16[512,6144]{1,0:T(8,128)(2,1)} %bitcast.6), custom_call_target="tpu_custom_call" | custom-call | tf_op jit(solution)/shard_map/pallas_call | solution.py:201
  118.6 1.5 %copy.12 = bf16[8,6144]{1,0:T(8,128)(2,1)} copy(bf16[8,6144]{1,0:T(8,128)(2,1)} %shard_map.64) | data formatting | bytes 196608
  (2 shorter events, 0.0 us)
Async XLA Ops:
  1.1 2.1 %copy-start = (s32[16]{0:T(128)}, s32[16]{0:T(128)S(1)}, u32[]{:S(2)}) copy-start(s32[16]{0:T(128)S(1)} %multiply_add_fusion.col_ref) | copy-start | bytes 196

commit v14 on v13

--- a/solution.py
+++ b/solution.py
@@ -59,15 +59,18 @@
     weight_copies[0].wait()
     weight_copies[1].wait()
 
+    pair = 2 if nx % 2 == 0 else 1
+
     def hidden_group(i, carry):
-        block = rows_ref[i].reshape(nz * rows, width)
+        lead = pl.ds(pl.multiple_of(i * pair, pair), pair)
+        block = rows_ref[lead].reshape(pair * nz * rows, width)
         gate = jnp.dot(block, wg[...], preferred_element_type=jnp.float32)
         up = jnp.dot(block, wu[...], preferred_element_type=jnp.float32)
         act = (jax.nn.silu(gate) * up).astype(hid.dtype)
-        hid[i] = act.reshape(nz, rows, hidden_width)
+        hid[lead] = act.reshape(pair, nz, rows, hidden_width)
         return carry
 
-    lax.fori_loop(0, nx, hidden_group, 0)
+    lax.fori_loop(0, nx // pair, hidden_group, 0)
     weight_copies[2].wait()
 
     rings = [("z", 1), ("z", -1), ("x", 1), ("x", -1)]

time: 120 us -> 120 us (level)
  no operation moved by 1% of the time
where the time goes in v14:
time: 120 us
  Pallas kernels  114 us (95%)
  local copies, waits for them, and re-layouts  4.8 us (4%)
    pallas_call x1, Pallas kernels, expert_reduce_scatter(): pl.pallas_call(functools.partial(rs_kernel, nsect, ny), out_shape=jax.Sha...  114 us
    unnamed x5, local copies, waits for them, and re-layouts  3.64 us

profile of v14, /device:TPU:1, one launch (start us, length us, event | category | flops | bytes accessed | tf_op | source)
XLA Modules:
  0.0 119.8 jit_solution(11862676948878327188)
XLA Ops:
  0.0 0.8 copy.9
  0.8 0.1 reshape.15
  0.8 0.1 fusion.1
  0.9 0.2 select_reduce_fusion
  1.1 0.0 copy-start
  1.2 1.0 broadcast_in_dim.2
  2.2 0.1 reshape.16
  2.2 1.0 convolution_convert_fusion.slab_ref
  3.2 0.0 copy-done
  3.2 1.3 %copy.10.logits_ref = f32[8,2]{1,0:T(8,128)} copy(f32[8,2]{0,1:T(2,128)} %param.7) | data formatting | bytes 128 | tf_op args[1]
  4.6 113.7 %shard_map.64 = bf16[8,6144]{1,0:T(8,128)(2,1)} custom-call(s32[16]{0:T(128)} %copy-done, f32[8,2]{1,0:T(8,128)} %copy.10.logits_ref, bf16[32,6144]{1,0:T(8,128)(2,1)} %convolution_convert_fusion.slab_ref, bf16[6144,512]{1,0:T(8,128)(2,1)} %bitcast.4, bf16[6144,512]{1,0:T(8,128)(2,1)} %bitcast.5, bf16[512,6144]{1,0:T(8,128)(2,1)} %bitcast.6), custom_call_target="tpu_custom_call" | custom-call | tf_op jit(solution)/shard_map/pallas_call | solution.py:204
  118.2 1.5 %copy.12 = bf16[8,6144]{1,0:T(8,128)(2,1)} copy(bf16[8,6144]{1,0:T(8,128)(2,1)} %shard_map.64) | data formatting | bytes 196608
  (2 shorter events, 0.0 us)
Async XLA Ops:
  1.1 2.1 %copy-start = (s32[16]{0:T(128)}, s32[16]{0:T(128)S(1)}, u32[]{:S(2)}) copy-start(s32[16]{0:T(128)S(1)} %multiply_add_fusion.col_ref) | copy-start | bytes 196

commit v15 on v14

--- a/solution.py
+++ b/solution.py
@@ -183,14 +183,11 @@
         local.wait()
     for cp in returns:
         cp.wait_recv()
-    logits = logits_ref[...]
-    gap = logits[:, 1:2] - logits[:, 0:1]
-    w_first = 1.0 / (1.0 + jnp.exp(gap))
-    w_second = 1.0 / (1.0 + jnp.exp(-gap))
     for t in range(mix_ref.shape[0]):
+        gap = jnp.full((1, width), logits_ref[2 * t + 1] - logits_ref[2 * t], jnp.float32)
         first = out_ref[pl.ds(col_ref[2 * t], 1), :]
         second = out_ref[pl.ds(col_ref[2 * t + 1], 1), :]
-        mix = w_first[t : t + 1] * first + w_second[t : t + 1] * second
+        mix = first / (1.0 + jnp.exp(gap)) + second / (1.0 + jnp.exp(-gap))
         mix_ref[pl.ds(t, 1), :] = mix.astype(mix_ref.dtype)
     for cp in copies1 + copies2 + returns:
         cp.wait_send()
@@ -206,7 +203,7 @@
         out_shape=jax.ShapeDtypeStruct((columns.shape[0] // 2, width), jnp.bfloat16),
         in_specs=[
             pl.BlockSpec(memory_space=pltpu.SMEM),
-            pl.BlockSpec(memory_space=pltpu.VMEM),
+            pl.BlockSpec(memory_space=pltpu.SMEM),
             pl.BlockSpec(memory_space=pltpu.VMEM),
             pl.BlockSpec(memory_space=pl.ANY),
             pl.BlockSpec(memory_space=pl.ANY),
@@ -375,13 +372,13 @@
     flat_ids, slot_rank = place_slots(expert_ids, experts_all)
     columns = flat_ids * capacity + slot_rank
     positions = jnp.arange(experts_all * capacity, dtype=jnp.int32)
-    picker = (positions[:, None] == columns[None, :]).astype(jnp.bfloat16)
-    repeated = jnp.repeat(tokens, 2, axis=0)
-    slab = jnp.dot(picker, repeated, preferred_element_type=jnp.float32).astype(jnp.bfloat16)
+    source = columns.reshape(token_count, 2)
+    picker = (positions[:, None, None] == source[None, :, :]).any(axis=2).astype(jnp.bfloat16)
+    slab = jnp.dot(picker, tokens, preferred_element_type=jnp.float32).astype(jnp.bfloat16)
     nx = lax.axis_size("ex")
     return expert_reduce_scatter(
         columns.astype(jnp.int32),
-        router_logits,
+        router_logits.reshape(-1),
         slab,
         w_gate[0],
         w_up[0],

time: 120 us -> 120 us (level)
    unnamed x5 -> x3, local copies, waits for them, and re-layouts: 3.64 us -> 3.05 us
where the time goes in v15:
time: 120 us
  Pallas kernels  113 us (94%)
  local copies, waits for them, and re-layouts  3.91 us (3%)
  matrix products  1.94 us (2%)
    pallas_call x1, Pallas kernels, expert_reduce_scatter(): pl.pallas_call(functools.partial(rs_kernel, nsect, ny), out_shape=jax.Sha...  113 us
    unnamed x3, local copies, waits for them, and re-layouts  3.05 us

profile of v15, /device:TPU:1, one launch (start us, length us, event | category | flops | bytes accessed | tf_op | source)
XLA Modules:
  0.0 120.1 jit_solution(9814606066607148722)
XLA Ops:
  0.0 0.8 copy.13
  0.8 0.1 reshape.13
  0.8 0.8 copy.14
  1.6 0.6 reshape.14.logits_ref
  2.2 0.1 fusion
  2.3 0.2 select_reduce_fusion
  2.5 0.5 multiply_add_fusion.1.col_ref
  3.0 0.1 reduce_sum.12
  3.1 0.1 copy.16
  3.2 0.1 fusion.1
  3.3 1.9 %convolution_convert_fusion.slab_ref = bf16[32,6144]{1,0:T(8,128)(2,1)} fusion(pred[32,8]{0,1:T(8,128)(4,1)S(1)} %fusion.1, bf16[8,6144]{1,0:T(8,128)(2,1)} %param.6), kind=kOutput, calls=%fused_computation | convolution fusion | flops 3342336 | bytes 491776 | tf_op jit(solution)/shard_map/dot_general | solution.py:377
  5.2 113.4 %shard_map.64 = bf16[8,6144]{1,0:T(8,128)(2,1)} custom-call(s32[16]{0:T(128)} %multiply_add_fusion.1.col_ref, f32[16]{0:T(128)} %reshape.14.logits_ref, bf16[32,6144]{1,0:T(8,128)(2,1)} %convolution_convert_fusion.slab_ref, bf16[6144,512]{1,0:T(8,128)(2,1)} %bitcast.5, bf16[6144,512]{1,0:T(8,128)(2,1)} %bitcast.6, bf16[512,6144]{1,0:T(8,128)(2,1)} %bitcast.7), custom_call_target="tpu_custom_call" | custom-call | tf_op jit(solution)/shard_map/pallas_call | solution.py:201
  118.6 1.5 %copy.18 = bf16[8,6144]{1,0:T(8,128)(2,1)} copy(bf16[8,6144]{1,0:T(8,128)(2,1)} %shard_map.64) | data formatting | bytes 196608
  (2 shorter events, 0.0 us)

commit v16 on v15

--- a/solution.py
+++ b/solution.py
@@ -98,56 +98,58 @@
     def other(axis):
         return "x" if axis == "z" else "z"
 
-    def both_sides(axis_of, own, stage_d, stage_f, recv_d, recv_f, recv_s, send, recv, finish):
-        copies = []
-        pending = {}
-        for r in range(4):
-            axis, d = axis_of(r), rings[r][1]
+    class Exchange:
+        def __init__(self, axis_of, own, stage_d, stage_f, recv_d, recv_f, recv_s, send, recv, finish):
+            self.axis_of, self.own = axis_of, own
+            self.stage_d, self.stage_f = stage_d, stage_f
+            self.recv_d, self.recv_f, self.recv_s = recv_d, recv_f, recv_s
+            self.send, self.recv, self.finish = send, recv, finish
+            self.copies, self.pending = [], {}
+
+        def begin(self, r):
+            axis, d = self.axis_of(r), rings[r][1]
             n = size_on(axis)
             me = me_on(axis)
-            stage_d[r] = own(r, lax.rem(me + n + d, n)).astype(stage_d.dtype)
+            self.stage_d[r] = self.own(r, lax.rem(me + n + d, n)).astype(self.stage_d.dtype)
             direct = pltpu.make_async_remote_copy(
-                src_ref=stage_d.at[r], dst_ref=recv_d.at[r], send_sem=send.at[r, 0],
-                recv_sem=recv.at[r, 0], device_id=dev(axis, d), device_id_type=MESH_ID,
+                src_ref=self.stage_d.at[r], dst_ref=self.recv_d.at[r], send_sem=self.send.at[r, 0],
+                recv_sem=self.recv.at[r, 0], device_id=dev(axis, d), device_id_type=MESH_ID,
             )
             direct.start()
-            stage_f[r] = own(r, lax.rem(me + 2 * n - 2 * d, n)).astype(stage_f.dtype)
+            self.stage_f[r] = self.own(r, lax.rem(me + 2 * n - 2 * d, n)).astype(self.stage_f.dtype)
             forward = pltpu.make_async_remote_copy(
-                src_ref=stage_f.at[r], dst_ref=recv_f.at[r], send_sem=send.at[r, 1],
-                recv_sem=recv.at[r, 1], device_id=dev(axis, -d), device_id_type=MESH_ID,
+                src_ref=self.stage_f.at[r], dst_ref=self.recv_f.at[r], send_sem=self.send.at[r, 1],
+                recv_sem=self.recv.at[r, 1], device_id=dev(axis, -d), device_id_type=MESH_ID,
             )
             forward.start()
-            pending[r] = (direct, forward)
-            copies += [direct, forward]
-        for r in range(4):
-            axis, d = axis_of(r), rings[r][1]
+            self.pending[r] = (direct, forward)
+            self.copies += [direct, forward]
+
+        def middle(self, r):
+            axis, d = self.axis_of(r), rings[r][1]
             n = size_on(axis)
             me = me_on(axis)
-            term = own(r, lax.rem(me + n - d, n))
-            pending[r][1].wait_recv()
-            recv_f[r] = (recv_f[r].astype(jnp.float32) + term).astype(recv_f.dtype)
+            term = self.own(r, lax.rem(me + n - d, n))
+            self.pending[r][1].wait_recv()
+            self.recv_f[r] = (self.recv_f[r].astype(jnp.float32) + term).astype(self.recv_f.dtype)
             second = pltpu.make_async_remote_copy(
-                src_ref=recv_f.at[r], dst_ref=recv_s.at[r], send_sem=send.at[r, 2],
-                recv_sem=recv.at[r, 2], device_id=dev(axis, -d), device_id_type=MESH_ID,
+                src_ref=self.recv_f.at[r], dst_ref=self.recv_s.at[r], send_sem=self.send.at[r, 2],
+                recv_sem=self.recv.at[r, 2], device_id=dev(axis, -d), device_id_type=MESH_ID,
             )
             second.start()
-            pending[r] = (pending[r][0], second)
-            copies.append(second)
-        for r in range(4):
-            axis = axis_of(r)
-            term = own(r, me_on(axis))
-            pending[r][0].wait_recv()
-            pending[r][1].wait_recv()
-            finish(r, term + recv_d[r].astype(jnp.float32) + recv_s[r].astype(jnp.float32))
-        return copies
+            self.pending[r] = (self.pending[r][0], second)
+            self.copies.append(second)
+
+        def end(self, r):
+            term = self.own(r, me_on(self.axis_of(r)))
+            self.pending[r][0].wait_recv()
+            self.pending[r][1].wait_recv()
+            self.finish(
+                r, term + self.recv_d[r].astype(jnp.float32) + self.recv_s[r].astype(jnp.float32)
+            )
 
     def keep_total1(r, value):
         total1[r] = value
-
-    copies1 = both_sides(
-        lambda r: rings[r][0], chunk, stage, stage_f1, s1.at[:, 0], s1.at[:, 1], s1.at[:, 2],
-        send1, recv1, keep_total1,
-    )
 
     def other_axis(r):
         return other(rings[r][0])
@@ -174,10 +176,26 @@
             cp.start()
             returns.append(cp)
 
-    copies2 = both_sides(
+    first_phase = Exchange(
+        lambda r: rings[r][0], chunk, stage, stage_f1, s1.at[:, 0], s1.at[:, 1], s1.at[:, 2],
+        send1, recv1, keep_total1,
+    )
+    second_phase = Exchange(
         other_axis, lambda r, j: total1[r, j], stage2_d, stage2_f, s2.at[:, 0], s2.at[:, 1], s2.at[:, 2],
         send2, recv2, keep_fin,
     )
+    for r in range(4):
+        first_phase.begin(r)
+    for r in range(4):
+        first_phase.middle(r)
+    for r in range(4):
+        first_phase.end(r)
+        second_phase.begin(r)
+    for r in range(4):
+        second_phase.middle(r)
+    for r in range(4):
+        second_phase.end(r)
+    copies1, copies2 = first_phase.copies, second_phase.copies
 
     for local in locals_:
         local.wait()

time: 120 us -> 119 us (level)
    pallas_call x1, Pallas kernels: 113 us -> 112 us  [expert_reduce_scatter(): pl.pallas_call(functools.partial(rs_kernel, nsect, ny), out_shape=jax.Sha...]
where the time goes in v16:
time: 119 us
  Pallas kernels  112 us (94%)
  local copies, waits for them, and re-layouts  3.91 us (3%)
  matrix products  1.94 us (2%)
    pallas_call x1, Pallas kernels, expert_reduce_scatter(): pl.pallas_call(functools.partial(rs_kernel, nsect, ny), out_shape=jax.Sha...  112 us
    unnamed x3, local copies, waits for them, and re-layouts  3.05 us

profile of v16, /device:TPU:1, one launch (start us, length us, event | category | flops | bytes accessed | tf_op | source)
XLA Modules:
  0.0 118.6 jit_solution(15228007331577940612)
XLA Ops:
  0.0 0.8 copy.13
  0.8 0.1 reshape.13
  0.8 0.8 copy.14
  1.6 0.6 reshape.14.logits_ref
  2.2 0.1 fusion
  2.3 0.2 select_reduce_fusion
  2.5 0.5 multiply_add_fusion.1.col_ref
  3.0 0.1 reduce_sum.12
  3.1 0.1 copy.16
  3.2 0.1 fusion.1
  3.3 1.9 %convolution_convert_fusion.slab_ref = bf16[32,6144]{1,0:T(8,128)(2,1)} fusion(pred[32,8]{0,1:T(8,128)(4,1)S(1)} %fusion.1, bf16[8,6144]{1,0:T(8,128)(2,1)} %param.6), kind=kOutput, calls=%fused_computation | convolution fusion | flops 3342336 | bytes 491776 | tf_op jit(solution)/shard_map/dot_general | solution.py:395
  5.2 111.8 %shard_map.64 = bf16[8,6144]{1,0:T(8,128)(2,1)} custom-call(s32[16]{0:T(128)} %multiply_add_fusion.1.col_ref, f32[16]{0:T(128)} %reshape.14.logits_ref, bf16[32,6144]{1,0:T(8,128)(2,1)} %convolution_convert_fusion.slab_ref, bf16[6144,512]{1,0:T(8,128)(2,1)} %bitcast.5, bf16[6144,512]{1,0:T(8,128)(2,1)} %bitcast.6, bf16[512,6144]{1,0:T(8,128)(2,1)} %bitcast.7), custom_call_target="tpu_custom_call" | custom-call | tf_op jit(solution)/shard_map/pallas_call | solution.py:219
  117.0 1.5 %copy.18 = bf16[8,6144]{1,0:T(8,128)(2,1)} copy(bf16[8,6144]{1,0:T(8,128)(2,1)} %shard_map.64) | data formatting | bytes 196608
  (2 shorter events, 0.0 us)

commit v17 on v16

--- a/solution.py
+++ b/solution.py
@@ -323,45 +323,57 @@
     def me_on(axis):
         return mz if axis == "z" else mx
 
-    def both_sides(axis_of, view, send, recv):
-        copies = []
-        first = {}
-        for r in range(4):
-            axis, d = axis_of(r), rings[r][1]
-            me = me_on(axis)
-            src = view(axis, r, me)
+    class Broadcast:
+        def __init__(self, axis_of, view, send, recv):
+            self.axis_of, self.view, self.send, self.recv = axis_of, view, send, recv
+            self.copies, self.first, self.later = [], {}, {}
+
+        def begin(self, r):
+            axis, d = self.axis_of(r), rings[r][1]
+            src = self.view(axis, r, me_on(axis))
             for side, sign in ((0, d), (1, -d)):
                 cp = pltpu.make_async_remote_copy(
-                    src_ref=src, dst_ref=src, send_sem=send.at[r, side], recv_sem=recv.at[r, side],
-                    device_id=dev(axis, sign), device_id_type=MESH_ID,
+                    src_ref=src, dst_ref=src, send_sem=self.send.at[r, side],
+                    recv_sem=self.recv.at[r, side], device_id=dev(axis, sign), device_id_type=MESH_ID,
                 )
                 cp.start()
-                first[(r, side)] = cp
-                copies.append(cp)
-        later = {}
-        for r in range(4):
-            axis, d = axis_of(r), rings[r][1]
+                self.first[(r, side)] = cp
+                self.copies.append(cp)
+
+        def middle(self, r):
+            axis, d = self.axis_of(r), rings[r][1]
             n = nz if axis == "z" else nx
-            first[(r, 1)].wait_recv()
-            passing = view(axis, r, lax.rem(me_on(axis) + n + d, n))
+            self.first[(r, 1)].wait_recv()
+            passing = self.view(axis, r, lax.rem(me_on(axis) + n + d, n))
             cp = pltpu.make_async_remote_copy(
-                src_ref=passing, dst_ref=passing, send_sem=send.at[r, 2], recv_sem=recv.at[r, 2],
-                device_id=dev(axis, -d), device_id_type=MESH_ID,
+                src_ref=passing, dst_ref=passing, send_sem=self.send.at[r, 2],
+                recv_sem=self.recv.at[r, 2], device_id=dev(axis, -d), device_id_type=MESH_ID,
             )
             cp.start()
-            later[r] = cp
-            copies.append(cp)
-        for r in range(4):
-            first[(r, 0)].wait_recv()
-            later[r].wait_recv()
-        return copies
-
-    copies1 = both_sides(lambda r: rings[r][0], block, send1, recv1)
+            self.later[r] = cp
+            self.copies.append(cp)
+
+        def end(self, r):
+            self.first[(r, 0)].wait_recv()
+            self.later[r].wait_recv()
 
     def second(r):
         return "x" if rings[r][0] == "z" else "z"
 
-    copies2 = both_sides(second, plane_block, send2, recv2)
+    first_phase = Broadcast(lambda r: rings[r][0], block, send1, recv1)
+    second_phase = Broadcast(second, plane_block, send2, recv2)
+    for r in range(4):
+        first_phase.begin(r)
+    for r in range(4):
+        first_phase.middle(r)
+    for r in range(4):
+        first_phase.end(r)
+        second_phase.begin(r)
+    for r in range(4):
+        second_phase.middle(r)
+    for r in range(4):
+        second_phase.end(r)
+    copies1, copies2 = first_phase.copies, second_phase.copies
     for cp in copies1 + copies2 + dispatch:
         cp.wait_send()
 

time: 119 us -> 120 us (level)
  no operation moved by 1% of the time
where the time goes in v17:
time: 120 us; the launch traced here: 119 us
  Pallas kernels  113 us (94%)
  local copies, waits for them, and re-layouts  3.91 us (3%)
  matrix products  1.94 us (2%)
    pallas_call x1, Pallas kernels, expert_reduce_scatter(): pl.pallas_call(functools.partial(rs_kernel, nsect, ny), out_shape=jax.Sha...  113 us
    unnamed x3, local copies, waits for them, and re-layouts  3.05 us

profile of v17, /device:TPU:1, one launch (start us, length us, event | category | flops | bytes accessed | tf_op | source)
XLA Modules:
  0.0 119.4 jit_solution(12107240232186607080)
XLA Ops:
  0.0 0.8 copy.13
  0.8 0.1 reshape.13
  0.8 0.8 copy.14
  1.6 0.6 reshape.14.logits_ref
  2.2 0.1 fusion
  2.3 0.2 select_reduce_fusion
  2.5 0.5 multiply_add_fusion.1.col_ref
  3.0 0.1 reduce_sum.12
  3.1 0.1 copy.16
  3.2 0.1 fusion.1
  3.3 1.9 %convolution_convert_fusion.slab_ref = bf16[32,6144]{1,0:T(8,128)(2,1)} fusion(pred[32,8]{0,1:T(8,128)(4,1)S(1)} %fusion.1, bf16[8,6144]{1,0:T(8,128)(2,1)} %param.6), kind=kOutput, calls=%fused_computation | convolution fusion | flops 3342336 | bytes 491776 | tf_op jit(solution)/shard_map/dot_general | solution.py:407
  5.2 112.7 %shard_map.64 = bf16[8,6144]{1,0:T(8,128)(2,1)} custom-call(s32[16]{0:T(128)} %multiply_add_fusion.1.col_ref, f32[16]{0:T(128)} %reshape.14.logits_ref, bf16[32,6144]{1,0:T(8,128)(2,1)} %convolution_convert_fusion.slab_ref, bf16[6144,512]{1,0:T(8,128)(2,1)} %bitcast.5, bf16[6144,512]{1,0:T(8,128)(2,1)} %bitcast.6, bf16[512,6144]{1,0:T(8,128)(2,1)} %bitcast.7), custom_call_target="tpu_custom_call" | custom-call | tf_op jit(solution)/shard_map/pallas_call | solution.py:219
  117.9 1.5 %copy.18 = bf16[8,6144]{1,0:T(8,128)(2,1)} copy(bf16[8,6144]{1,0:T(8,128)(2,1)} %shard_map.64) | data formatting | bytes 196608
  (2 shorter events, 0.0 us)

commit v18 on v16

--- a/solution.py
+++ b/solution.py
@@ -59,7 +59,7 @@
     weight_copies[0].wait()
     weight_copies[1].wait()
 
-    pair = 2 if nx % 2 == 0 else 1
+    pair = nx
 
     def hidden_group(i, carry):
         lead = pl.ds(pl.multiple_of(i * pair, pair), pair)

time: 119 us -> 119 us (level)
  no operation moved by 1% of the time
where the time goes in v18:
time: 119 us; the launch traced here: 118 us
  Pallas kernels  112 us (94%)
  local copies, waits for them, and re-layouts  3.91 us (3%)
  matrix products  1.94 us (2%)
    pallas_call x1, Pallas kernels, expert_reduce_scatter(): pl.pallas_call(functools.partial(rs_kernel, nsect, ny), out_shape=jax.Sha...  112 us
    unnamed x3, local copies, waits for them, and re-layouts  3.05 us

profile of v18, /device:TPU:1, one launch (start us, length us, event | category | flops | bytes accessed | tf_op | source)
XLA Modules:
  0.0 118.4 jit_solution(15614357793505826285)
XLA Ops:
  0.0 0.8 copy.13
  0.8 0.1 reshape.13
  0.8 0.8 copy.14
  1.6 0.6 reshape.14.logits_ref
  2.2 0.1 fusion
  2.3 0.2 select_reduce_fusion
  2.5 0.5 multiply_add_fusion.1.col_ref
  3.0 0.1 reduce_sum.12
  3.1 0.1 copy.16
  3.2 0.1 fusion.1
  3.3 1.9 %convolution_convert_fusion.slab_ref = bf16[32,6144]{1,0:T(8,128)(2,1)} fusion(pred[32,8]{0,1:T(8,128)(4,1)S(1)} %fusion.1, bf16[8,6144]{1,0:T(8,128)(2,1)} %param.6), kind=kOutput, calls=%fused_computation | convolution fusion | flops 3342336 | bytes 491776 | tf_op jit(solution)/shard_map/dot_general | solution.py:395
  5.2 111.6 %shard_map.64 = bf16[8,6144]{1,0:T(8,128)(2,1)} custom-call(s32[16]{0:T(128)} %multiply_add_fusion.1.col_ref, f32[16]{0:T(128)} %reshape.14.logits_ref, bf16[32,6144]{1,0:T(8,128)(2,1)} %convolution_convert_fusion.slab_ref, bf16[6144,512]{1,0:T(8,128)(2,1)} %bitcast.5, bf16[6144,512]{1,0:T(8,128)(2,1)} %bitcast.6, bf16[512,6144]{1,0:T(8,128)(2,1)} %bitcast.7), custom_call_target="tpu_custom_call" | custom-call | tf_op jit(solution)/shard_map/pallas_call | solution.py:219
  116.9 1.5 %copy.18 = bf16[8,6144]{1,0:T(8,128)(2,1)} copy(bf16[8,6144]{1,0:T(8,128)(2,1)} %shard_map.64) | data formatting | bytes 196608
  (2 shorter events, 0.0 us)

commit v19 on v16

--- a/solution.py
+++ b/solution.py
@@ -110,18 +110,18 @@
             axis, d = self.axis_of(r), rings[r][1]
             n = size_on(axis)
             me = me_on(axis)
+            self.stage_f[r] = self.own(r, lax.rem(me + 2 * n - 2 * d, n)).astype(self.stage_f.dtype)
+            forward = pltpu.make_async_remote_copy(
+                src_ref=self.stage_f.at[r], dst_ref=self.recv_f.at[r], send_sem=self.send.at[r, 1],
+                recv_sem=self.recv.at[r, 1], device_id=dev(axis, -d), device_id_type=MESH_ID,
+            )
+            forward.start()
             self.stage_d[r] = self.own(r, lax.rem(me + n + d, n)).astype(self.stage_d.dtype)
             direct = pltpu.make_async_remote_copy(
                 src_ref=self.stage_d.at[r], dst_ref=self.recv_d.at[r], send_sem=self.send.at[r, 0],
                 recv_sem=self.recv.at[r, 0], device_id=dev(axis, d), device_id_type=MESH_ID,
             )
             direct.start()
-            self.stage_f[r] = self.own(r, lax.rem(me + 2 * n - 2 * d, n)).astype(self.stage_f.dtype)
-            forward = pltpu.make_async_remote_copy(
-                src_ref=self.stage_f.at[r], dst_ref=self.recv_f.at[r], send_sem=self.send.at[r, 1],
-                recv_sem=self.recv.at[r, 1], device_id=dev(axis, -d), device_id_type=MESH_ID,
-            )
-            forward.start()
             self.pending[r] = (direct, forward)
             self.copies += [direct, forward]
 
@@ -330,7 +330,7 @@
             axis, d = axis_of(r), rings[r][1]
             me = me_on(axis)
             src = view(axis, r, me)
-            for side, sign in ((0, d), (1, -d)):
+            for side, sign in ((1, -d), (0, d)):
                 cp = pltpu.make_async_remote_copy(
                     src_ref=src, dst_ref=src, send_sem=send.at[r, side], recv_sem=recv.at[r, side],
                     device_id=dev(axis, sign), device_id_type=MESH_ID,

time: 119 us -> 119 us (level)
  no operation moved by 1% of the time
where the time goes in v19:
time: 119 us
  Pallas kernels  112 us (94%)
  local copies, waits for them, and re-layouts  3.91 us (3%)
  matrix products  1.94 us (2%)
    pallas_call x1, Pallas kernels, expert_reduce_scatter(): pl.pallas_call(functools.partial(rs_kernel, nsect, ny), out_shape=jax.Sha...  112 us
    unnamed x3, local copies, waits for them, and re-layouts  3.05 us

profile of v19, /device:TPU:1, one launch (start us, length us, event | category | flops | bytes accessed | tf_op | source)
XLA Modules:
  0.0 119.0 jit_solution(12075260306967205921)
XLA Ops:
  0.0 0.8 copy.13
  0.8 0.1 reshape.13
  0.8 0.8 copy.14
  1.6 0.6 reshape.14.logits_ref
  2.2 0.1 fusion
  2.3 0.2 select_reduce_fusion
  2.5 0.5 multiply_add_fusion.1.col_ref
  3.0 0.1 reduce_sum.12
  3.1 0.1 copy.16
  3.2 0.1 fusion.1
  3.3 1.9 %convolution_convert_fusion.slab_ref = bf16[32,6144]{1,0:T(8,128)(2,1)} fusion(pred[32,8]{0,1:T(8,128)(4,1)S(1)} %fusion.1, bf16[8,6144]{1,0:T(8,128)(2,1)} %param.6), kind=kOutput, calls=%fused_computation | convolution fusion | flops 3342336 | bytes 491776 | tf_op jit(solution)/shard_map/dot_general | solution.py:395
  5.2 112.2 %shard_map.64 = bf16[8,6144]{1,0:T(8,128)(2,1)} custom-call(s32[16]{0:T(128)} %multiply_add_fusion.1.col_ref, f32[16]{0:T(128)} %reshape.14.logits_ref, bf16[32,6144]{1,0:T(8,128)(2,1)} %convolution_convert_fusion.slab_ref, bf16[6144,512]{1,0:T(8,128)(2,1)} %bitcast.5, bf16[6144,512]{1,0:T(8,128)(2,1)} %bitcast.6, bf16[512,6144]{1,0:T(8,128)(2,1)} %bitcast.7), custom_call_target="tpu_custom_call" | custom-call | tf_op jit(solution)/shard_map/pallas_call | solution.py:219
  117.4 1.5 %copy.18 = bf16[8,6144]{1,0:T(8,128)(2,1)} copy(bf16[8,6144]{1,0:T(8,128)(2,1)} %shard_map.64) | data formatting | bytes 196608
  (2 shorter events, 0.0 us)
